TPU v7x, 256 devices: a whole 4x4x8 slice. The times are simulated.
256 devices in a mesh: det: 64 (over x, z, core), row: 4 (over y).
Axes of the slice: x: 4, y: 4, z: 8, core: 2. Of those that a mesh axis runs over, the one named last changes fastest.
Arguments:
- images: bfloat16 [384, 3, 384, 384], P('det', None, 'row'), may hold values from -6 to 6
- warp_rows: bfloat16 [384, 3, 384, 384], P('det', None, 'row'), may hold values from -0.3125 to 0.3125
- warp_cols: bfloat16 [384, 3, 384, 384], P('det'), may hold values from -0.3125 to 0.3125
- psf_coef: float32 [384, 3, 21], P('det'), may hold values from -1.25 to 1.25
- taps: float32 [21, 21], replicated, may hold values from -1.25 to 1.25
- dest_patch: int32 [3456, 1], replicated, may hold values from 0 to 63; in each aligned block of 54 rows (0 to 53, 54 to 107, ...) at most 2 rows name the same one
- dest_block: int32 [3456], replicated, may hold values from 0 to 2
- weight_index: int32 [384, 3], replicated, may hold values from 0 to 7
- weight_table: float32 [8], replicated, may hold values from 0.25 to 4
- patch_home: int32 [64], replicated, may hold values from 0 to 63, each once
Outputs:
- difference: bfloat16 [384, 3, 384, 384], P('det', None, 'row')
- coadd: bfloat16 [64, 384, 384], P('det', 'row')
Inputs may be any that keep to these rules, and one draw needn't show every extreme that they name: `dest_patch`: within the 54 rows of one device (an aligned block of rows), no patch is named more than 2 times. `patch_home`: each position once.
All inputs are finite; a program needn't handle non-finite values.
Results may differ from a plain program's by a relative error of at most 0.0082.
Values may be sent and summed in bfloat16 or wider, within the bound.
A program may use at most 128 MiB of HBM per device.

v0:
```python
import jax
import jax.numpy as jnp
from jax import lax
from jax.sharding import PartitionSpec as P

TILE = 128


def extended(value, sides, width):
    for axis, dim in sides:
        size, length = (lax.axis_size(axis), value.shape[dim])
        up = [(i, (i + 1) % size) for i in range(size - 1)]
        down = [(j, i) for i, j in up]
        last = lax.slice_in_dim(value, length - width, length, axis=dim)
        first = lax.slice_in_dim(value, 0, width, axis=dim)
        before = lax.ppermute(last, axis, up)
        after = lax.ppermute(first, axis, down)
        value = jnp.concatenate([before, value, after], axis=dim)
    return value


def toeplitz_table(values, out_len, in_len):
    span_len = values.shape[1]
    offsets = jnp.arange(in_len)[None, :] - jnp.arange(out_len)[:, None]
    picks = (offsets[:, :, None] == jnp.arange(span_len)[None, None, :]).astype(jnp.float32)
    return jnp.einsum("oij,kj->koi", picks, values.astype(jnp.float32)).astype(jnp.bfloat16)


def per_device(
    images,
    warp_rows,
    warp_cols,
    psf_coef,
    taps,
    dest_patch,
    dest_block,
    weight_index,
    weight_table,
    patch_home,
):
    det_count, visit_count, band_rows, side_cols = images.shape
    kernel_count, tap_count = taps.shape
    reach = (tap_count - 1) // 2
    tile_cols = TILE
    tile_count = side_cols // tile_cols
    det_devices = lax.axis_size("det")
    my_index = lax.axis_index("det")
    image_count = det_count * visit_count
    piece_count = image_count * tile_count
    capacity = max(2, 2 * ((piece_count + det_devices - 1) // det_devices))
    slot_count = det_devices * capacity
    padded_rows = band_rows + 2 * reach
    col_warped = jnp.einsum(
        "dvbs,dvst->dvbt", images, warp_cols, preferred_element_type=jnp.float32
    ).astype(jnp.bfloat16)
    warped = jnp.einsum(
        "dvbr,dvrs->dvbs",
        warp_rows,
        lax.all_gather(col_warped, "row", axis=2, tiled=True),
        preferred_element_type=jnp.float32,
    ).astype(jnp.bfloat16)
    padded = extended(warped, (("row", 2),), reach)
    taps_half = taps.astype(jnp.bfloat16)
    col_table = toeplitz_table(taps_half, tile_cols, tile_cols + 2 * reach)
    tiles_in = padded.reshape(image_count, padded_rows, side_cols)
    coef_rows = psf_coef.reshape(image_count, kernel_count)

    def match_image(inputs):
        tile_image, coef_row = inputs
        widened = jnp.pad(tile_image, ((0, 0), (reach, reach)))
        windows = jnp.stack(
            [
                widened[
                    :, column_tile * tile_cols : column_tile * tile_cols + tile_cols + 2 * reach
                ]
                for column_tile in range(tile_count)
            ],
            axis=1,
        )
        conv_cols = jnp.einsum(
            "rtw,kcw->krtc", windows, col_table, preferred_element_type=jnp.float32
        ).astype(jnp.bfloat16)
        conv_cols = conv_cols.reshape(kernel_count, padded_rows, side_cols)
        scaled = (coef_row[:, None] * taps).astype(jnp.bfloat16)
        row_table = toeplitz_table(scaled, band_rows, padded_rows)
        return jnp.einsum("kbr,krs->bs", row_table, conv_cols, preferred_element_type=jnp.float32)

    matched = lax.map(match_image, (tiles_in, coef_rows))
    level_count = weight_table.shape[0]
    level_onehot = (weight_index[:, :, None] == jnp.arange(level_count)[None, None, :]).astype(
        jnp.float32
    )
    weight_all = jnp.sum(level_onehot * weight_table[None, None, :], axis=2)
    weight_mine = lax.dynamic_slice_in_dim(weight_all, my_index * det_count, det_count, 0).reshape(
        image_count
    )
    weighted = (
        (weight_mine[:, None, None] * matched)
        .astype(jnp.bfloat16)
        .reshape(image_count, band_rows, tile_count, tile_cols)
    )
    patch_count = patch_home.shape[0]
    patch_ids = dest_patch[:, 0]
    owner_all = jnp.sum(
        jnp.where(patch_ids[:, None] == jnp.arange(patch_count)[None, :], patch_home[None, :], 0),
        axis=1,
    )
    owner_grid = owner_all.reshape(det_devices, piece_count)
    earlier = jnp.arange(piece_count)[None, :] < jnp.arange(piece_count)[:, None]
    rank_grid = jnp.sum(
        ((owner_grid[:, :, None] == owner_grid[:, None, :]) & earlier[None]).astype(jnp.int32),
        axis=2,
    )
    slot_grid = owner_grid * capacity + rank_grid
    slot_mine = lax.dynamic_slice_in_dim(slot_grid, my_index, 1, 0)[0]
    send_pick = (
        (jnp.arange(slot_count)[:, None] == slot_mine[None, :])
        .astype(jnp.bfloat16)
        .reshape(slot_count, image_count, tile_count)
    )
    weight_pieces = jnp.repeat(weight_all.reshape(-1), tile_count)
    to_mine = owner_all == my_index
    block_onehot = (dest_block[:, None] == jnp.arange(tile_count)[None, :]).astype(jnp.float32)
    denominator = jnp.sum(
        jnp.where(to_mine[:, None], block_onehot * weight_pieces[:, None], 0.0), axis=0
    )
    source_slot = jnp.arange(
        det_devices * piece_count
    ) // piece_count * capacity + rank_grid.reshape(-1)
    slot_onehot = (
        (source_slot[:, None] == jnp.arange(slot_count)[None, :]) & to_mine[:, None]
    ).astype(jnp.float32)
    gather_matrix = jnp.einsum("iq,is->qs", block_onehot, slot_onehot).astype(jnp.bfloat16)
    outgoing = jnp.einsum(
        "spq,pbqc->sbc", send_pick, weighted, preferred_element_type=jnp.float32
    ).astype(jnp.bfloat16)
    received = lax.all_to_all(outgoing, "det", split_axis=0, concat_axis=0, tiled=True)
    numerator = jnp.einsum(
        "qs,sbc->bqc", gather_matrix, received, preferred_element_type=jnp.float32
    )
    template = (numerator / jnp.maximum(denominator, 1.0)[None, :, None]).astype(jnp.bfloat16)
    coadd_band = template.reshape(1, band_rows, side_cols)
    returned = jnp.einsum(
        "qs,bqc->sbc", gather_matrix, template, preferred_element_type=jnp.float32
    ).astype(jnp.bfloat16)
    arrived = lax.all_to_all(returned, "det", split_axis=0, concat_axis=0, tiled=True)
    local_template = jnp.einsum(
        "spq,sbc->pbqc", send_pick, arrived, preferred_element_type=jnp.float32
    )
    difference = (
        matched.reshape(image_count, band_rows, tile_count, tile_cols) - local_template
    ).astype(jnp.bfloat16)
    difference = difference.reshape(det_count, visit_count, band_rows, side_cols)
    return (difference, coadd_band)


def solution(mesh):
    placed = (
        P("det", None, "row", None),
        P("det", None, "row", None),
        P("det", None, None, None),
        P("det", None, None),
        P(),
        P(),
        P(),
        P(),
        P(),
        P(),
    )
    return jax.shard_map(
        per_device,
        mesh=mesh,
        in_specs=placed,
        out_specs=(P("det", None, "row", None), P("det", "row", None)),
        check_vma=False,
    )
```

profile of v0, /device:TPU:1, one launch (start us, length us, event | category | flops | bytes accessed | tf_op | source)
XLA Modules:
  0.0 490.7 jit_solution(14183806398760456192)
XLA Ops:
  8.5 4.7 convolution_convert_fusion.3
  15.2 62.1 %all-gather.2.cloned.1.call-done = bf16[6,3,384,384]{3,2,1,0:T(8,128)(2,1)} async-done(((bf16[6,3,96,384]{3,2,1,0:T(8,128)(2,1)}), bf16[6,3,384,384]{3,2,1,0:T(8,128)(2,1)}) %all-gather.2.cloned.1.call-update) | async-done | bytes 5308432 | tf_op jit(solution)/shard_map/all_gather | solution.py:59
  77.3 3.6 fusion.26
  87.8 3.8 collective-permute-done.1
  93.4 198.1 %while.12 = (s32[]{:T(128)}, f32[18,96,384]{2,1,0:T(8,128)}, f32[18,21]{1,0:T(8,128)S(1)}, f32[21,21]{1,0:T(8,128)S(1)}, bf16[18,116,384]{2,1,0:T(8,128)(2,1)}, /*index=5*/bf16[21,128,148]{1,2,0:T(8,128)(2,1)}, s32[]{:T(128)}) while((s32[]{:T(128)}, f32[18,96,384]{2,1,0:T(8,128)}, f32[18,21]{1,0:T(8,128)S(1)}, f32[21,21]{1,0:T(8,128)S(1)}, ...), condition=%wide.region_1.2_spmd, body=%wide.region_0.1_spmd.sunk | while | flops 468033056 | bytes 10274817 | solution.py:88
  95.7 3.2 convert_bitcast_fusion.2
  106.7 3.2 convert_bitcast_fusion.2
  117.7 3.2 convert_bitcast_fusion.2
  128.7 3.2 convert_bitcast_fusion.2
  139.7 3.2 convert_bitcast_fusion.2
  150.7 3.2 convert_bitcast_fusion.2
  161.7 3.2 convert_bitcast_fusion.2
  172.7 3.2 convert_bitcast_fusion.2
  183.7 3.2 convert_bitcast_fusion.2
  194.7 3.2 convert_bitcast_fusion.2
  260.7 3.2 convert_bitcast_fusion.2
  294.5 3.6 reshape.134
  300.1 3.7 copy.71
  303.8 12.1 %all-to-all-start = ((bf16[128,96,128]{2,1,0:T(8,128)(2,1)}), bf16[128,96,128]{2,1,0:T(8,128)(2,1)}, u32[]{:S(2)}, u32[]{:S(2)}) async-start(bf16[128,96,128]{2,1,0:T(8,128)(2,1)} %copy.71), calls=%async_computation | async-start | bytes 6291456 | tf_op jit(solution)/shard_map/all_to_all | solution.py:137
  318.4 71.0 %all-to-all-done = bf16[128,96,128]{2,1,0:T(8,128)(2,1)} async-done(((bf16[128,96,128]{2,1,0:T(8,128)(2,1)}), bf16[128,96,128]{2,1,0:T(8,128)(2,1)}, u32[]{:S(2)}, u32[]{:S(2)}) %all-to-all-start) | async-done | bytes 3145760 | tf_op jit(solution)/shard_map/all_to_all | solution.py:137
  393.3 3.7 copy.74
  397.0 6.2 %all-to-all-start.1 = ((bf16[128,96,128]{2,1,0:T(8,128)(2,1)}), bf16[128,96,128]{2,1,0:T(8,128)(2,1)}, u32[]{:S(2)}, u32[]{:S(2)}) async-start(bf16[128,96,128]{2,1,0:T(8,128)(2,1)} %copy.74), calls=%async_computation.1 | async-start | bytes 6291456 | tf_op jit(solution)/shard_map/all_to_all | solution.py:146
  403.9 72.7 %all-to-all-done.1 = bf16[128,96,128]{2,1,0:T(8,128)(2,1)} async-done(((bf16[128,96,128]{2,1,0:T(8,128)(2,1)}), bf16[128,96,128]{2,1,0:T(8,128)(2,1)}, u32[]{:S(2)}, u32[]{:S(2)}) %all-to-all-start.1) | async-done | bytes 3145760 | tf_op jit(solution)/shard_map/all_to_all | solution.py:146
  476.7 3.3 fusion.15
  (215 shorter events, 190.0 us)
Async XLA Ops:
  7.2 1.3 copy-start
  7.2 6.1 %copy-start.9 = (f32[8]{0:T(128)S(1)}, f32[8]{0:T(128)}, u32[]{:S(2)}) copy-start(f32[8]{0:T(128)} %param.20) | copy-start | bytes 100
  7.2 6.1 %copy-start.7 = (s32[384,3]{0,1:T(4,128)S(1)}, s32[384,3]{0,1:T(4,128)}, u32[]{:S(2)}) copy-start(s32[384,3]{0,1:T(4,128)} %param.19) | copy-start | bytes 13828
  7.2 6.4 %copy-start.6 = (f32[6,3,21]{2,1,0:T(4,128)S(1)}, f32[6,3,21]{2,1,0:T(4,128)}, u32[]{:S(2)}) copy-start(f32[6,3,21]{2,1,0:T(4,128)} %param.15) | copy-start | bytes 4540
  7.2 6.4 %copy-start.5 = (s32[3456,1]{0,1:T(1,128)S(1)}, s32[3456,1]{0,1:T(1,128)}, u32[]{:S(2)}) copy-start(s32[3456,1]{0,1:T(1,128)} %param.17) | copy-start | bytes 41476
  7.2 6.5 %copy-start.8 = (s32[64]{0:T(128)S(1)}, s32[64]{0:T(128)}, u32[]{:S(2)}) copy-start(s32[64]{0:T(128)} %param.21) | copy-start | bytes 772
  7.2 70.1 %all-gather.2.cloned.1.call-start = ((), (), s32[]{:S(2)}) async-start(), calls=%async_computation.2 | async-start | bytes 6635520 | tf_op jit(solution)/shard_map/all_gather | solution.py:59
  13.2 64.1 %copy-start.2 = (bf16[6,3,96,384]{3,2,1,0:T(8,128)(2,1)S(1)}, bf16[6,3,96,384]{3,2,1,0:T(8,128)(2,1)}, u32[]{:S(2)}) copy-start(bf16[6,3,96,384]{3,2,1,0:T(8,128)(2,1)} %param.13) | copy-start | bytes 3981316
  15.2 69.8 %copy-start.3 = (f32[21,21]{1,0:T(8,128)S(1)}, f32[21,21]{1,0:T(8,128)}, u32[]{:S(2)}) copy-start(f32[21,21]{1,0:T(8,128)} %param.16) | copy-start | bytes 5296
  81.0 6.7 %collective-permute-start = (bf16[6,3,10,384]{3,2,1,0:T(8,128)(2,1)S(1)}, bf16[6,3,10,384]{3,2,1,0:T(8,128)(2,1)S(1)}, u32[]{:S(2)}, u32[]{:S(2)}) collective-permute-start(bf16[6,3,10,384]{3,2,1,0:T(8,128)(2,1)S(1)} %get-tuple-element.125), channel_id=1, source_target_pairs={{0,1},{1,2},{2,3},{4,5},{5,6},{6,7},{8,9},{9,10},{10,11},{12,13},{... | collective-permute-start | bytes 414728 | tf_op jit(solution)/shard_map/ppermute | solution.py:16
  83.7 7.9 %collective-permute-start.1 = (bf16[6,3,10,384]{3,2,1,0:T(8,128)(2,1)S(1)}, bf16[6,3,10,384]{3,2,1,0:T(8,128)(2,1)S(1)}, u32[]{:S(2)}, u32[]{:S(2)}) collective-permute-start(bf16[6,3,10,384]{3,2,1,0:T(8,128)(2,1)S(1)} %get-tuple-element.126), channel_id=1, source_target_pairs={{1,0},{2,1},{3,2},{5,4},{6,5},{7,6},{9,8},{10,9},{11,10},{13,12},{... | collective-permute-start | bytes 414728 | tf_op jit(solution)/shard_map/ppermute | solution.py:17
  303.8 13.3 %copy-start.4 = (s32[3456]{0:T(1024)S(1)}, s32[3456]{0:T(1024)}, u32[]{:S(2)}) copy-start(s32[3456]{0:T(1024)} %param.18) | copy-start | bytes 41476
  303.8 85.6 %all-to-all-start = ((bf16[128,96,128]{2,1,0:T(8,128)(2,1)}), bf16[128,96,128]{2,1,0:T(8,128)(2,1)}, u32[]{:S(2)}, u32[]{:S(2)}) async-start(bf16[128,96,128]{2,1,0:T(8,128)(2,1)} %copy.71), calls=%async_computation | async-start | bytes 6291456 | tf_op jit(solution)/shard_map/all_to_all | solution.py:137
  397.0 79.7 %all-to-all-start.1 = ((bf16[128,96,128]{2,1,0:T(8,128)(2,1)}), bf16[128,96,128]{2,1,0:T(8,128)(2,1)}, u32[]{:S(2)}, u32[]{:S(2)}) async-start(bf16[128,96,128]{2,1,0:T(8,128)(2,1)} %copy.74), calls=%async_computation.1 | async-start | bytes 6291456 | tf_op jit(solution)/shard_map/all_to_all | solution.py:146
  476.7 3.3 copy-start.1
Sparse Core Ops, SparseCore 0:
  13.4 63.8 all-gather.1
where the time goes:
time: 495 us; the launch traced here: 491 us
  waiting for transfers between devices  211 us (43%)
  matrix products  143 us (29%)
  local copies, waits for them, and re-layouts  92.9 us (19%)
  starting transfers between devices  22.4 us (5%)
  between operations  14.4 us (3%)
  other arithmetic  7.01 us (1%)
    all_to_all x1, waiting for transfers between devices, per_device(): lax.all_to_all(returned, 'det', split_axis=0, concat_axis=0, tiled=True)  72.7 us
    all_to_all x1, waiting for transfers between devices, per_device(): lax.all_to_all(outgoing, 'det', split_axis=0, concat_axis=0, tiled=True)  71 us
    all_gather x1, waiting for transfers between devices, per_device(): lax.all_gather(col_warped, 'row', axis=2, tiled=True)  62.1 us
    dot_general x18, matrix products, match_image(): jnp.einsum('rtw,kcw->krtc', windows, col_table, preferred_element_type=jn...  57.4 us
    convert_element_type x18, local copies, waits for them, and re-layouts, match_image(): conv_cols = jnp.einsum('rtw,kcw->krtc', windows, col_table, preferred_ele...  54.3 us
    dot_general x18, matrix products, match_image(): jnp.einsum('kbr,krs->bs', row_table, conv_cols, preferred_element_type=jn...  44.7 us
    dot_general x19, matrix products, toeplitz_table(): jnp.einsum('oij,kj->koi', picks, values.astype(jnp.float32))  22.1 us
    dynamic_slice x36, local copies, waits for them, and re-layouts, per_device(): matched = lax.map(match_image, (tiles_in, coef_rows))  18.7 us
  transfers between devices with their start and end apart: 5, of which 5 were waited for; matrix products, arithmetic and copies ran while one was open for 1% of the time, Pallas kernels for 0%

commit v1 on v0

v1 whole, which is shorter than its diff:
```python
import functools

import jax
import jax.numpy as jnp
from jax import lax
from jax.experimental import pallas as pl
from jax.experimental.pallas import tpu as pltpu
from jax.sharding import PartitionSpec as P

TILE = 128
HALF = 64
HALO = 16
GROUP = 4


def build_table(base_ref, image, keep, table_ref, offsets):
    for t in range(offsets - 2):
        row = jnp.broadcast_to(base_ref[image, pl.ds(t, 1), :], keep.shape)
        band = pltpu.roll(row, 0, 1, stride=1, stride_axis=0)
        band = jnp.where(keep, band, 0.0).astype(jnp.bfloat16)
        table_ref[pl.ds(t * TILE, keep.shape[0]), pl.ds(0, TILE)] = band
        table_ref[pl.ds((t + 2) * TILE, keep.shape[0]), pl.ds(TILE, TILE)] = band


def table_mask(span):
    rows = lax.broadcasted_iota(jnp.int32, (96, TILE), 0)
    lanes = lax.broadcasted_iota(jnp.int32, (96, TILE), 1)
    gap = rows - jnp.where(lanes >= HALF, lanes - HALF, lanes)
    return (gap >= 0) & (gap < span)


def convolve(warped, reach, window_ref, left_ref, table_ref, out_ref, image, offsets):
    rows, cols = warped.shape
    wide = jnp.concatenate([warped, jnp.zeros((rows, TILE), jnp.float32)], axis=1)
    even = pltpu.roll(wide, reach, 1)
    odd = pltpu.roll(wide, cols + TILE + reach - HALF, 1)
    tiles = cols // TILE
    groups = out_ref.shape[2] // GROUP
    for tile in range(tiles):
        window_ref[2 * tile] = even[:, tile * TILE : (tile + 1) * TILE]
        window_ref[2 * tile + 1] = odd[:, tile * TILE : (tile + 1) * TILE]
    for offset in range(offsets):
        start = HALO - reach + offset
        parts = [window_ref[w, pl.ds(start, groups, stride=GROUP), :] for w in range(2 * tiles)]
        left_ref[:, pl.ds(offset * TILE, TILE)] = jnp.concatenate(parts, axis=0).astype(jnp.bfloat16)
    product = jnp.dot(left_ref[...], table_ref[...], preferred_element_type=jnp.float32)
    low = lax.broadcasted_iota(jnp.int32, (groups, TILE), 1) < HALF
    for tile in range(tiles):
        for pair in range(2):
            first = product[(2 * tile) * groups : (2 * tile + 1) * groups, pair * TILE : (pair + 1) * TILE]
            second = product[(2 * tile + 1) * groups : (2 * tile + 2) * groups, pair * TILE : (pair + 1) * TILE]
            upper = jnp.where(low, first, pltpu.roll(second, HALF, 1))
            lower = jnp.where(low, pltpu.roll(first, HALF, 1), second)
            out_ref[image, tile, pl.ds(2 * pair, groups, stride=GROUP), :] = upper
            out_ref[image, tile, pl.ds(2 * pair + 1, groups, stride=GROUP), :] = lower


def match_kernel(reach, offsets, base_ref, rows_ref, full_ref, out_ref, window_ref, left_ref, table_ref):
    @pl.when(pl.program_id(0) == 0)
    def _():
        table_ref[...] = jnp.zeros_like(table_ref)

    build_table(base_ref, 0, table_mask(2 * reach + 1), table_ref, offsets)
    warped = jnp.dot(rows_ref[0], full_ref[0], preferred_element_type=jnp.float32)
    convolve(warped, reach, window_ref, left_ref, table_ref, out_ref, 0, offsets)


def match(base, rows_ext, full, reach):
    images, ext, cols = rows_ext.shape
    band = ext - 2 * HALO
    offsets = 2 * reach + GROUP
    return pl.pallas_call(
        functools.partial(match_kernel, reach, offsets),
        grid=(images,),
        in_specs=[
            pl.BlockSpec((1,) + base.shape[1:], lambda i: (i, 0, 0)),
            pl.BlockSpec((1, ext, cols), lambda i: (i, 0, 0)),
            pl.BlockSpec((1, cols, cols), lambda i: (i, 0, 0)),
        ],
        out_specs=pl.BlockSpec((1, cols // TILE, band, TILE), lambda i: (i, 0, 0, 0)),
        out_shape=jax.ShapeDtypeStruct((images, cols // TILE, band, TILE), jnp.float32),
        scratch_shapes=[
            pltpu.VMEM((2 * (cols // TILE), ext, TILE), jnp.float32),
            pltpu.VMEM((2 * (cols // TILE) * (band // GROUP), offsets * TILE), jnp.bfloat16),
            pltpu.VMEM((offsets * TILE, 2 * TILE), jnp.bfloat16),
        ],
        compiler_params=pltpu.CompilerParams(vmem_limit_bytes=48 << 20),
        name="match",
    )(base, rows_ext, full)


def collect_kernel(tiles, target_ref, weight_ref, matched_ref, dense_ref):
    image = pl.program_id(0)

    @pl.when(image == 0)
    def _():
        dense_ref[...] = jnp.zeros_like(dense_ref)

    for tile in range(tiles):
        piece = weight_ref[image] * matched_ref[0, tile]
        piece = piece.astype(jnp.bfloat16).astype(jnp.float32)
        target = target_ref[image * tiles + tile]
        dense_ref[target] = (dense_ref[target].astype(jnp.float32) + piece).astype(jnp.bfloat16)


def collect(targets, weights, matched, boxes):
    images, tiles, band, _ = matched.shape
    return pl.pallas_call(
        functools.partial(collect_kernel, tiles),
        grid_spec=pltpu.PrefetchScalarGridSpec(
            num_scalar_prefetch=2,
            grid=(images,),
            in_specs=[pl.BlockSpec((1, tiles, band, TILE), lambda i, *_: (i, 0, 0, 0))],
            out_specs=pl.BlockSpec((boxes, band, TILE), lambda i, *_: (0, 0, 0), pipeline_mode=pl.Buffered(1)),
        ),
        out_shape=jax.ShapeDtypeStruct((boxes, band, TILE), jnp.bfloat16),
        compiler_params=pltpu.CompilerParams(vmem_limit_bytes=32 << 20),
        name="collect",
    )(targets, weights, matched)


def subtract_kernel(tiles, target_ref, matched_ref, template_ref, out_ref):
    image = pl.program_id(0)
    for tile in range(tiles):
        target = target_ref[image * tiles + tile]
        lanes = pl.ds(tile * TILE, TILE)
        out_ref[0, :, lanes] = (matched_ref[0, tile] - template_ref[target].astype(jnp.float32)).astype(jnp.bfloat16)


def subtract(targets, matched, templates):
    images, tiles, band, _ = matched.shape
    return pl.pallas_call(
        functools.partial(subtract_kernel, tiles),
        grid_spec=pltpu.PrefetchScalarGridSpec(
            num_scalar_prefetch=1,
            grid=(images,),
            in_specs=[
                pl.BlockSpec((1, tiles, band, TILE), lambda i, *_: (i, 0, 0, 0)),
                pl.BlockSpec(templates.shape, lambda i, *_: (0, 0, 0), pipeline_mode=pl.Buffered(1)),
            ],
            out_specs=pl.BlockSpec((1, band, tiles * TILE), lambda i, *_: (i, 0, 0)),
        ),
        out_shape=jax.ShapeDtypeStruct((images, band, tiles * TILE), jnp.bfloat16),
        compiler_params=pltpu.CompilerParams(vmem_limit_bytes=32 << 20),
        name="subtract",
    )(targets, matched, templates)


def base_rows(psf_coef, taps):
    images = psf_coef.shape[0]
    kernels, span = taps.shape
    scaled = (psf_coef[:, :, None] * taps[None]).astype(jnp.bfloat16)
    by_tap = jnp.transpose(scaled, (0, 2, 1))
    lead = jnp.pad(by_tap, ((0, 0), (0, 1), (0, 0)))
    late = jnp.pad(by_tap, ((0, 0), (1, 0), (0, 0)))
    both = jnp.concatenate([lead, late], axis=2)
    lanes = jnp.arange(TILE)[None, :]
    taken = jnp.arange(span)[:, None]
    here = ((-taken) % TILE == lanes).astype(jnp.float32)
    there = (HALF - taken == lanes).astype(jnp.float32)
    half = taps.astype(jnp.bfloat16).astype(jnp.float32)
    placed = jnp.concatenate(
        [
            jnp.dot(half, here, precision=lax.Precision.HIGHEST),
            jnp.dot(half, there, precision=lax.Precision.HIGHEST),
        ],
        axis=0,
    ).astype(jnp.bfloat16)
    return jnp.einsum("itk,kc->itc", both, placed, preferred_element_type=jnp.float32)


def per_device(
    images,
    warp_rows,
    warp_cols,
    psf_coef,
    taps,
    dest_patch,
    dest_block,
    weight_index,
    weight_table,
    patch_home,
):
    dets, visits, band, cols = images.shape
    reach = (taps.shape[1] - 1) // 2
    tiles = cols // TILE
    count = dets * visits
    patches = patch_home.shape[0]
    me = lax.axis_index("det")
    row_size = lax.axis_size("row")

    rows = warp_rows.reshape(count, band, cols)
    up = [(i, i + 1) for i in range(row_size - 1)]
    down = [(j, i) for i, j in up]
    before = lax.ppermute(rows[:, band - HALO :], "row", up)
    after = lax.ppermute(rows[:, :HALO], "row", down)
    rows_ext = jnp.concatenate([before, rows, after], axis=1)
    col_warped = jnp.einsum(
        "nbs,nst->nbt",
        images.reshape(count, band, cols),
        warp_cols.reshape(count, cols, cols),
        preferred_element_type=jnp.float32,
    ).astype(jnp.bfloat16)
    full = lax.all_gather(col_warped, "row", axis=1, tiled=True)

    base = base_rows(psf_coef.reshape(count, -1), taps)
    matched = match(base, rows_ext, full, reach)

    levels = weight_table.shape[0]
    flat_index = weight_index.reshape(-1)
    weight_all = jnp.sum(
        jnp.where(flat_index[:, None] == jnp.arange(levels)[None, :], weight_table[None, :], 0.0), axis=1
    )
    weight_mine = lax.dynamic_slice_in_dim(weight_all, me * count, count, 0)
    patch_mine = lax.dynamic_slice_in_dim(dest_patch[:, 0], me * count * tiles, count * tiles, 0)
    block_mine = lax.dynamic_slice_in_dim(dest_block, me * count * tiles, count * tiles, 0)
    home_mine = jnp.sum(
        jnp.where(patch_mine[:, None] == jnp.arange(patches)[None, :], patch_home[None, :], 0), axis=1
    )
    targets = home_mine * tiles + block_mine
    my_patch = jnp.sum(jnp.where(patch_home == me, jnp.arange(patches), 0))
    to_mine = jnp.where(dest_patch[:, 0] == my_patch, dest_block, -1).reshape(-1, tiles)
    denominator = jnp.stack(
        [jnp.sum(jnp.where(to_mine == b, weight_all[:, None], 0.0)) for b in range(tiles)]
    )

    dense = collect(targets, weight_mine, matched, patches * tiles)
    numerator = lax.psum_scatter(dense, "det", scatter_dimension=0, tiled=True)
    template = (numerator.astype(jnp.float32) / jnp.maximum(denominator, 1.0)[:, None, None]).astype(jnp.bfloat16)
    coadd = jnp.transpose(template, (1, 0, 2)).reshape(1, band, cols)
    templates = lax.all_gather(template, "det", axis=0, tiled=True)
    difference = subtract(targets, matched, templates)
    return (difference.reshape(dets, visits, band, cols), coadd)


def solution(mesh):
    placed = (
        P("det", None, "row", None),
        P("det", None, "row", None),
        P("det", None, None, None),
        P("det", None, None),
        P(),
        P(),
        P(),
        P(),
        P(),
        P(),
    )
    return jax.shard_map(
        per_device,
        mesh=mesh,
        in_specs=placed,
        out_specs=(P("det", None, "row", None), P("det", "row", None)),
        check_vma=False,
    )
```

time: 495 us -> 346 us (0.70)
  matrix products: 143 us -> 5.36 us
  local copies, waits for them, and re-layouts: 92.9 us -> 12.7 us
  waiting for transfers between devices: 211 us -> 271 us
  Pallas kernels: 0 us -> 26.3 us
  starting transfers between devices: 22.4 us -> 6.76 us
    all_to_all x2 -> x0, waiting for transfers between devices: 144 us -> none  [the longest x1 72.7 us: per_device(): lax.all_to_all(returned, 'det', split_axis=0, concat_axis=0, tiled=True)]
    dot_general x62 -> x4, matrix products: 143 us -> 5.36 us  [the longest x1 4.71 us: per_device(): jnp.einsum('nbs,nst->nbt', images.reshape(count, band, cols), warp_cols.r...]
    reduce_scatter x0 -> x1, waiting for transfers between devices: none -> 136 us  [per_device(): numerator = lax.psum_scatter(dense, 'det', scatter_dimension=0, tiled=True)]
    all_gather x1 -> x2, waiting for transfers between devices: 62.1 us -> 135 us  [the longest x1 83.4 us: per_device(): templates = lax.all_gather(template, 'det', axis=0, tiled=True)]
    convert_element_type x21 -> x0, local copies, waits for them, and re-layouts: 62.6 us -> none  [the longest x18 54.3 us: match_image(): conv_cols = jnp.einsum('rtw,kcw->krtc', windows, col_table, preferred_ele...]
    pallas_call x0 -> x3, Pallas kernels: none -> 26.3 us  [the longest x1 17.9 us: match(): pl.pallas_call(functools.partial(match_kernel, reach, offsets), grid=(ima...]
    dynamic_slice x38 -> x1, local copies, waits for them, and re-layouts: 18.8 us -> 0.08 us  [per_device(): weight_mine = lax.dynamic_slice_in_dim(weight_all, me * count, count, 0)]
    all_to_all x2 -> x0, starting transfers between devices: 18.4 us -> none  [the longest x1 12.1 us: per_device(): lax.all_to_all(outgoing, 'det', split_axis=0, concat_axis=0, tiled=True)]
  transfers between devices with their start and end apart: 5 -> 5, of which waited for: 5 -> 3; matrix products, arithmetic and copies ran while one was open for 1% -> 3% of each run, Pallas kernels for 0% -> 0%
where the time goes in v1:
time: 346 us; the launch traced here: 345 us
  waiting for transfers between devices  271 us (78%)
  Pallas kernels  26.3 us (8%)
  between operations  13.9 us (4%)
  local copies, waits for them, and re-layouts  12.7 us (4%)
  other arithmetic  9.32 us (3%)
  starting transfers between devices  6.76 us (2%)
  matrix products  5.36 us (2%)
    reduce_scatter x1, waiting for transfers between devices, per_device(): numerator = lax.psum_scatter(dense, 'det', scatter_dimension=0, tiled=True)  136 us
    all_gather x1, waiting for transfers between devices, per_device(): templates = lax.all_gather(template, 'det', axis=0, tiled=True)  83.4 us
    all_gather x1, waiting for transfers between devices, per_device(): full = lax.all_gather(col_warped, 'row', axis=1, tiled=True)  51.5 us
    pallas_call x1, Pallas kernels, match(): pl.pallas_call(functools.partial(match_kernel, reach, offsets), grid=(ima...  17.9 us
    unnamed x27, local copies, waits for them, and re-layouts  9.19 us
  transfers between devices with their start and end apart: 5, of which 3 were waited for; matrix products, arithmetic and copies ran while one was open for 3% of the time, Pallas kernels for 0%

profile of v1, /device:TPU:1, one launch (start us, length us, event | category | flops | bytes accessed | tf_op | source)
XLA Modules:
  0.0 345.1 jit_solution(7312629991509347761)
XLA Ops:
  7.2 1.3 copy-done
  8.5 4.7 %convolution_convert_fusion = bf16[18,96,384]{2,1,0:T(8,128)(2,1)} fusion(bf16[18,96,384]{2,1,0:T(8,128)(2,1)S(1)} %bitcast.21, bf16[18,384,384]{2,1,0:T(8,128)(2,1)} %bitcast.22), kind=kOutput, calls=%fused_computation.1 | convolution fusion | flops 510271488 | bytes 7962624 | tf_op jit(solution)/shard_map/nbs,nst->nbt/dot_general | solution.py:198
  13.3 1.1 fusion.23
  14.4 1.3 collective-permute-start.1
  15.7 5.3 %collective-permute-start = (bf16[18,16,384]{2,1,0:T(8,128)(2,1)S(1)}, bf16[18,16,384]{2,1,0:T(8,128)(2,1)}, u32[]{:S(2)}, u32[]{:S(2)}) collective-permute-start(bf16[18,16,384]{2,1,0:T(8,128)(2,1)S(1)} %get-tuple-element.5), channel_id=1, source_target_pairs={{0,1},{1,2},{2,3},{4,5},{5,6},{6,7},{8,9},{9,10},{10,11},{12,13},{... | collective-permute-start | bytes 663560 | tf_op jit(solution)/shard_map/ppermute | solution.py:195
  21.7 0.8 dynamic-slice_bitcast_fusion
  23.4 0.8 dynamic-slice_add_fusion.target_ref
  24.1 1.6 pad_maximum_fusion.rows_ref
  25.8 51.5 %all-gather.3.cloned.1.call-done.full_ref = bf16[18,384,384]{2,1,0:T(8,128)(2,1)} async-done(((bf16[18,96,384]{2,1,0:T(8,128)(2,1)}), bf16[18,384,384]{2,1,0:T(8,128)(2,1)}) %all-gather.3.cloned.1.call-update) | async-done | bytes 5308432 | tf_op jit(solution)/shard_map/all_gather | solution.py:204
  77.3 17.9 %match.1.matched_ref = f32[18,3,96,128]{3,2,1,0:T(8,128)S(1)} custom-call(f32[18,22,128]{2,1,0:T(8,128)S(1)} %fusion.5.base_ref, bf16[18,128,384]{2,1,0:T(8,128)(2,1)S(1)} %pad_maximum_fusion.rows_ref, bf16[18,384,384]{2,1,0:T(8,128)(2,1)} %all-gather.3.cloned.1.call-done.full_ref), custom_call_target="tpu_custom_call" | custom-call | tf_op jit(solution)/shard_map/match/pallas_call | solution.py:72
  95.2 2.0 collect.1
  97.2 1.5 copy-done.1
  98.7 2.1 copy-done.3
  102.1 0.7 compare_reduce_fusion
  102.8 0.7 select_reduce_fusion.4
  103.5 2.0 maximum_maximum_fusion
  105.6 135.8 %reduce-scatter.2.cloned.1.call-done = bf16[3,96,128]{2,1,0:T(8,128)(2,1)} async-done(((bf16[192,96,128]{2,1,0:T(8,128)(2,1)}), bf16[3,96,128]{2,1,0:T(8,128)(2,1)}) %reduce-scatter.2.cloned.1.call-update) | async-done | bytes 73744 | tf_op jit(solution)/shard_map/reduce_scatter | solution.py:228
  241.3 1.6 divide_convert_fusion
  242.9 1.0 fusion.26
  244.0 0.7 reshape.89
  244.7 83.4 %all-gather.5.cloned.1.call-done.template_ref = bf16[192,96,128]{2,1,0:T(8,128)(2,1)} async-done(((bf16[3,96,128]{2,1,0:T(8,128)(2,1)}), bf16[192,96,128]{2,1,0:T(8,128)(2,1)}) %all-gather.5.cloned.1.call-update) | async-done | bytes 4718608 | tf_op jit(solution)/shard_map/all_gather | solution.py:231
  328.1 1.7 copy-done.2
  329.8 2.3 copy-done.4
  332.1 6.5 %subtract.1 = bf16[18,96,384]{2,1,0:T(8,128)(2,1)} custom-call(s32[54]{0:T(128)S(1)} %dynamic-slice_add_fusion.target_ref, f32[18,3,96,128]{3,2,1,0:T(8,128)S(1)} %copy-done.2, bf16[192,96,128]{2,1,0:T(8,128)(2,1)S(1)} %copy-done.4), custom_call_target="tpu_custom_call" | custom-call | tf_op jit(solution)/shard_map/subtract/pallas_call | solution.py:132
  (46 shorter events, 2.9 us)
Async XLA Ops:
  7.2 1.3 copy-start
  7.2 70.1 %all-gather.3.cloned.1.call-start = ((), (), s32[]{:S(2)}) async-start(), calls=%async_computation.1 | async-start | bytes 6635520 | tf_op jit(solution)/shard_map/all_gather | solution.py:204
  13.2 7.9 %copy-start.8 = (f32[21,21]{1,0:T(8,128)S(1)}, f32[21,21]{1,0:T(8,128)}, u32[]{:S(2)}) copy-start(f32[21,21]{1,0:T(8,128)} %param.14) | copy-start | bytes 5296
  13.2 7.9 %copy-start.7 = (f32[6,3,21]{2,1,0:T(4,128)S(1)}, f32[6,3,21]{2,1,0:T(4,128)}, u32[]{:S(2)}) copy-start(f32[6,3,21]{2,1,0:T(4,128)} %param.13) | copy-start | bytes 4540
  13.2 8.0 %copy-start.9 = (s32[384,3]{0,1:T(4,128)S(1)}, s32[384,3]{0,1:T(4,128)}, u32[]{:S(2)}) copy-start(s32[384,3]{0,1:T(4,128)} %param.17) | copy-start | bytes 13828
  13.2 8.3 %copy-start.10 = (f32[8]{0:T(128)S(1)}, f32[8]{0:T(128)}, u32[]{:S(2)}) copy-start(f32[8]{0:T(128)} %param.18) | copy-start | bytes 100
  13.2 9.3 %copy-start.11 = (s32[64]{0:T(128)S(1)}, s32[64]{0:T(128)}, u32[]{:S(2)}) copy-start(s32[64]{0:T(128)} %param.19) | copy-start | bytes 772
  13.2 228.1 %reduce-scatter.2.cloned.1.call-start = ((), (), s32[]{:S(2)}) async-start(), calls=%async_computation.2 | async-start | bytes 4792320 | tf_op jit(solution)/shard_map/reduce_scatter | solution.py:228
  14.4 9.7 %collective-permute-start.1 = (bf16[18,16,384]{2,1,0:T(8,128)(2,1)S(1)}, bf16[18,16,384]{2,1,0:T(8,128)(2,1)S(1)}, u32[]{:S(2)}, u32[]{:S(2)}) collective-permute-start(bf16[18,16,384]{2,1,0:T(8,128)(2,1)S(1)} %get-tuple-element.6), channel_id=1, source_target_pairs={{1,0},{2,1},{3,2},{5,4},{6,5},{7,6},{9,8},{10,9},{11,10},{13,12},{... | collective-permute-start | bytes 663560 | tf_op jit(solution)/shard_map/ppermute | solution.py:196
  15.7 8.4 %collective-permute-start = (bf16[18,16,384]{2,1,0:T(8,128)(2,1)S(1)}, bf16[18,16,384]{2,1,0:T(8,128)(2,1)}, u32[]{:S(2)}, u32[]{:S(2)}) collective-permute-start(bf16[18,16,384]{2,1,0:T(8,128)(2,1)S(1)} %get-tuple-element.5), channel_id=1, source_target_pairs={{0,1},{1,2},{2,3},{4,5},{5,6},{6,7},{8,9},{9,10},{10,11},{12,13},{... | collective-permute-start | bytes 663560 | tf_op jit(solution)/shard_map/ppermute | solution.py:195
  97.2 1.5 copy-start.1
  98.7 2.1 copy-start.3
  100.8 0.7 copy-start.12
  100.8 1.3 copy-start.6
  100.8 2.0 copy-start.5
  100.9 227.2 %all-gather.5.cloned.1.call-start = ((), (), s32[]{:S(2)}) async-start(), calls=%async_computation.3 | async-start | bytes 4792320 | tf_op jit(solution)/shard_map/all_gather | solution.py:231
  328.1 1.7 copy-start.2
  329.8 2.3 copy-start.4
Sparse Core Ops, SparseCore 0:
  13.4 63.8 all-gather.2
  101.0 140.2 reduce-scatter.1
  244.6 83.3 all-gather.4

commit v2 on v1

--- a/solution.py
+++ b/solution.py
@@ -11,6 +11,8 @@
 HALF = 64
 HALO = 16
 GROUP = 4
+DEPTH = 8
+SPLIT = 128
 
 
 def build_table(base_ref, image, keep, table_ref, offsets):
@@ -146,6 +148,300 @@
     )(targets, matched, templates)
 
 
+def det_index(x, z, core, depth):
+    return (x * depth + z) * 2 + core
+
+
+class Links:
+    def __init__(self, send_ref, recv_ref):
+        self.send_ref, self.recv_ref = send_ref, recv_ref
+        self.copies = {}
+
+    def start(self, key, source, target, device):
+        index = len(self.copies)
+        copy = pltpu.make_async_remote_copy(
+            src_ref=source,
+            dst_ref=target,
+            send_sem=self.send_ref.at[index],
+            recv_sem=self.recv_ref.at[index],
+            device_id=device,
+            device_id_type=pl.DeviceIdType.MESH,
+        )
+        copy.start()
+        self.copies[key] = copy
+
+    def arrive(self, key):
+        self.copies[key].wait_recv()
+
+    def finish(self):
+        for copy in self.copies.values():
+            copy.wait_send()
+
+
+def signed(place, step, way, size):
+    return lax.rem(place + size + (step if way == 0 else -step), size)
+
+
+def ring_reduce(links, tag, size, place, lead, rows, at, held_ref, whole_ref, half_ref, neighbour, base, finish):
+    middle, half = size // 2, rows // 2
+
+    def add(dest, extras, store):
+        if base is not None:
+            base(dest)
+
+        def body(l, carry):
+            for lo in (0, half):
+                index = at(dest, l, lo, half)
+                total = held_ref[index].astype(jnp.float32)
+                if base is not None:
+                    total = total + base.ref[base.index(dest, l, lo, half)].astype(jnp.float32)
+                for ref, way, from_half in extras:
+                    if not from_half:
+                        total = total + ref[way, l, pl.ds(lo, half), :].astype(jnp.float32)
+                    elif lo == way * half:
+                        total = total + ref[way, l].astype(jnp.float32)
+                store(l, lo, index, total)
+            return carry
+
+        lax.fori_loop(0, lead, body, 0)
+
+    def put(l, lo, index, total):
+        held_ref[index] = total.astype(jnp.bfloat16)
+
+    far = signed(place, middle, 0, size)
+    if base is not None:
+        add(far, [], put)
+    for way in (0, 1):
+        links.start((tag, way, middle), held_ref.at[at(far, None, way * half, half)], half_ref.at[way], neighbour(way))
+    yield
+    for step in range(middle - 1, 0, -1):
+        for way in (0, 1):
+            dest = signed(place, step, way, size)
+            links.arrive((tag, way, step + 1))
+            source = (half_ref, way, True) if step + 1 == middle else (whole_ref.at[step], way, False)
+            add(dest, [source], put)
+            links.start(
+                (tag, way, step), held_ref.at[at(dest, None, 0, rows)], whole_ref.at[step - 1, way], neighbour(way)
+            )
+        yield
+    for way in (0, 1):
+        links.arrive((tag, way, 1))
+    add(place, [(whole_ref.at[0], 0, False), (whole_ref.at[0], 1, False)], put if finish is None else finish)
+    yield
+
+
+def ring_gather(links, tag, size, place, rows, view, neighbour, arrived):
+    middle, half = size // 2, rows // 2
+    for way in (0, 1):
+        links.start((tag, way, 1), view(place, 0, rows), view(place, 0, rows), neighbour(way))
+    arrived(place, 0)
+    yield
+    for step in range(1, middle):
+        for way in (0, 1):
+            origin = signed(place, step, 1 - way, size)
+            links.arrive((tag, way, step))
+            lo, length = (0, rows) if step + 1 < middle else (way * half, half)
+            links.start((tag, way, step + 1), view(origin, lo, length), view(origin, lo, length), neighbour(way))
+            arrived(origin, (step, way))
+        yield
+    for way in (0, 1):
+        links.arrive((tag, way, middle))
+    arrived(signed(place, middle, 0, size), middle)
+    yield
+
+
+def exchange_kernel(
+    width,
+    depth,
+    split,
+    total_ref,
+    dense_ref,
+    all_ref,
+    coadd_ref,
+    held_ref,
+    az_ref,
+    az_half,
+    ax_ref,
+    ax_half,
+    bx_ref,
+    bx_half,
+    bz_ref,
+    bz_half,
+    send_ref,
+    recv_ref,
+):
+    rows = dense_ref.shape[3]
+    band = coadd_ref.shape[0]
+    me = lax.axis_index("det")
+    core = lax.rem(me, 2)
+    z = lax.rem(me // 2, depth)
+    x = me // (2 * depth)
+    other = {"det": det_index(x, z, 1 - core, depth)}
+    beside = [{"det": det_index(signed(x, 1, way, width), z, core, depth)} for way in (0, 1)]
+    along = [{"det": det_index(x, signed(z, 1, way, depth), core, depth)} for way in (0, 1)]
+    barrier = pltpu.get_barrier_semaphore()
+    friends = [other] + beside + along
+    for friend in friends:
+        pl.semaphore_signal(barrier, inc=1, device_id=friend, device_id_type=pl.DeviceIdType.MESH)
+    pl.semaphore_wait(barrier, len(friends))
+
+    links = Links(send_ref, recv_ref)
+    rest = rows - split
+
+    def everything(l, size):
+        return pl.ds(0, size) if l is None else l
+
+    def a_at(dest, l, lo, length):
+        return (everything(l, width), dest, pl.ds(lo, length), slice(None))
+
+    def b_at(dest, l, lo, length):
+        return (dest, everything(l, depth), pl.ds(split + lo, length), slice(None))
+
+    def a_next(dest, l, lo, length):
+        return (pl.ds(dest, 1) if l is None else dest, z, pl.ds(lo, length), slice(None))
+
+    def b_next(dest, l, lo, length):
+        return (pl.ds(x, 1) if l is None else x, dest, pl.ds(split + lo, length), slice(None))
+
+    def with_core(index, which):
+        return index[:2] + (which,) + index[2:]
+
+    def hand_over(tag, dest, at, length):
+        index = at(dest, None, 0, length)
+        links.start(tag, dense_ref.at[with_core(index, 1 - core)], held_ref.at[index], other)
+
+    zs = [(depth // 2, 0)] + [(s, w) for s in range(depth // 2 - 1, 0, -1) for w in (0, 1)] + [(0, 0)]
+    xs = [(width // 2, 0)] + [(s, w) for s in range(width // 2 - 1, 0, -1) for w in (0, 1)] + [(0, 0)]
+    turns = [("b", xs[0]), ("a", zs[0]), ("a", zs[1]), ("a", zs[2])]
+    turns += [("b", k) for k in xs[1:-1]] + [("a", k) for k in zs[3:]] + [("b", xs[-1])]
+    for part, (step, way) in turns:
+        if part == "a":
+            hand_over(("core a", step, way), signed(z, step, way, depth), a_at, split)
+        else:
+            hand_over(("core b", step, way), signed(x, step, way, width), b_at, rest)
+
+    def base_of(tag, order, at):
+        left = list(order)
+
+        def base(dest):
+            step, way = left.pop(0)
+            links.arrive((tag, step, way))
+
+        base.ref = dense_ref
+        base.index = lambda *key: with_core(at(*key), core)
+        return base
+
+    def divided(offset):
+        def store(l, lo, index, total):
+            start, end = offset + lo, offset + lo + total.shape[0]
+            while start < end:
+                box = start // band
+                stop = min(end, (box + 1) * band)
+                part = total[start - offset - lo : stop - offset - lo] / jnp.maximum(total_ref[box], 1.0)
+                part = part.astype(jnp.bfloat16)
+                all_ref[x, z, core, pl.ds(start, stop - start), :] = part
+                coadd_ref[pl.ds(start - box * band, stop - start), pl.ds(box * TILE, TILE)] = part
+                start = stop
+
+        return store
+
+    a_first = ring_reduce(
+        links, "a z", depth, z, width, split, a_at, held_ref, az_ref, az_half, lambda w: along[w],
+        base_of("core a", zs, a_at), None,
+    )
+    b_first = ring_reduce(
+        links, "b x", width, x, depth, rest, b_at, held_ref, bx_ref, bx_half, lambda w: beside[w],
+        base_of("core b", xs, b_at), None,
+    )
+    a_second = ring_reduce(
+        links, "a x", width, x, 1, split, a_next, held_ref, ax_ref, ax_half, lambda w: beside[w], None, divided(0)
+    )
+    b_second = ring_reduce(
+        links, "b z", depth, z, 1, rest, b_next, held_ref, bz_ref, bz_half, lambda w: along[w], None, divided(split)
+    )
+
+    def a_view(origin, lo, length):
+        return all_ref.at[:, origin, core, pl.ds(lo, length), :]
+
+    def b_view(origin, lo, length):
+        return all_ref.at[origin, :, core, pl.ds(split + lo, length), :]
+
+    def a_own(origin, lo, length):
+        return all_ref.at[origin, z, core, pl.ds(lo, length), :]
+
+    def b_own(origin, lo, length):
+        return all_ref.at[x, origin, core, pl.ds(split + lo, length), :]
+
+    def nothing(origin, key):
+        return None
+
+    def across(tag, view, length):
+        def arrived(origin, key):
+            links.start((tag, key), view(origin, 0, length), view(origin, 0, length), other)
+
+        return arrived
+
+    a_third = ring_gather(links, "a gather x", width, x, split, a_own, lambda w: beside[w], nothing)
+    b_third = ring_gather(links, "b gather z", depth, z, rest, b_own, lambda w: along[w], nothing)
+    a_last = ring_gather(
+        links, "a gather z", depth, z, split, a_view, lambda w: along[w], across("core a back", a_view, split)
+    )
+    b_last = ring_gather(
+        links, "b gather x", width, x, rest, b_view, lambda w: beside[w], across("core b back", b_view, rest)
+    )
+
+    def chain(*parts):
+        for part in parts:
+            yield from part
+
+    a_run = chain(a_first, a_second, a_third, a_last)
+    b_run = chain(b_first, b_second, b_third, b_last)
+    order = "ba" "a" "b" "aa" "ba" "baba" "bab" "bab" "abab" "b" "aabaabaab"
+    runs = {"a": a_run, "b": b_run}
+    for name in order:
+        next(runs[name], None)
+    for run in runs.values():
+        for _ in run:
+            pass
+    for key in list(links.copies):
+        if key[0] in ("core a back", "core b back"):
+            links.arrive(key)
+    links.finish()
+
+
+def exchange(totals, dense, width, depth, split):
+    rows = dense.shape[3]
+    band = rows // totals.shape[0]
+    rest = rows - split
+    copies = 2 * (2 * width + 2 * depth + 4) + 16
+
+    def buffers(size, lead, length):
+        return [
+            pltpu.VMEM((size // 2 - 1, 2, lead, length, TILE), jnp.bfloat16),
+            pltpu.VMEM((2, lead, length // 2, TILE), jnp.bfloat16),
+        ]
+
+    return pl.pallas_call(
+        functools.partial(exchange_kernel, width, depth, split),
+        in_specs=[pl.BlockSpec(memory_space=pltpu.SMEM), pl.BlockSpec(memory_space=pltpu.VMEM)],
+        out_specs=[pl.BlockSpec(memory_space=pltpu.VMEM)] * 2,
+        out_shape=[
+            jax.ShapeDtypeStruct(dense.shape, jnp.bfloat16),
+            jax.ShapeDtypeStruct((band, totals.shape[0] * TILE), jnp.bfloat16),
+        ],
+        scratch_shapes=[pltpu.VMEM((width, depth, rows, TILE), jnp.bfloat16)]
+        + buffers(depth, width, split)
+        + buffers(width, 1, split)
+        + buffers(width, depth, rest)
+        + buffers(depth, 1, rest)
+        + [pltpu.SemaphoreType.DMA((copies,)), pltpu.SemaphoreType.DMA((copies,))],
+        compiler_params=pltpu.CompilerParams(
+            collective_id=0, has_side_effects=True, vmem_limit_bytes=40 << 20
+        ),
+        name="exchange",
+    )(totals, dense)
+
+
 def base_rows(psf_coef, taps):
     images = psf_coef.shape[0]
     kernels, span = taps.shape
@@ -225,12 +521,13 @@
     )
 
     dense = collect(targets, weight_mine, matched, patches * tiles)
-    numerator = lax.psum_scatter(dense, "det", scatter_dimension=0, tiled=True)
-    template = (numerator.astype(jnp.float32) / jnp.maximum(denominator, 1.0)[:, None, None]).astype(jnp.bfloat16)
-    coadd = jnp.transpose(template, (1, 0, 2)).reshape(1, band, cols)
-    templates = lax.all_gather(template, "det", axis=0, tiled=True)
+    depth = DEPTH
+    width = patches // (2 * depth)
+    shape = (width, depth, 2, tiles * band, TILE)
+    templates, coadd = exchange(denominator, dense.reshape(shape), width, depth, SPLIT)
+    templates = templates.reshape(patches * tiles, band, TILE)
     difference = subtract(targets, matched, templates)
-    return (difference.reshape(dets, visits, band, cols), coadd)
+    return (difference.reshape(dets, visits, band, cols), coadd[None])
 
 
 def solution(mesh):

time: 346 us -> 190 us (0.55)
  waiting for transfers between devices: 271 us -> 49.5 us
  Pallas kernels: 26.3 us -> 104 us
  local copies, waits for them, and re-layouts: 12.7 us -> 4.23 us
    reduce_scatter x1 -> x0, waiting for transfers between devices: 136 us -> none  [per_device(): numerator = lax.psum_scatter(dense, 'det', scatter_dimension=0, tiled=True)]
    all_gather x1 -> x0, waiting for transfers between devices: 83.4 us -> none  [per_device(): templates = lax.all_gather(template, 'det', axis=0, tiled=True)]
    pallas_call x0 -> x1, Pallas kernels: none -> 77.9 us  [exchange(): pl.pallas_call(functools.partial(exchange_kernel, width, depth, split), i...]
    unnamed x27 -> x18, local copies, waits for them, and re-layouts: 9.19 us -> 2.08 us
  transfers between devices with their start and end apart: 5 -> 3, of which waited for: 3 -> 2; matrix products, arithmetic and copies ran while one was open for 3% -> 5% of each run, Pallas kernels for 0% -> 0%
where the time goes in v2:
time: 190 us; the launch traced here: 189 us
  Pallas kernels  104 us (55%)
  waiting for transfers between devices  49.5 us (26%)
  between operations  14.2 us (7%)
  other arithmetic  6.07 us (3%)
  starting transfers between devices  5.37 us (3%)
  matrix products  5.36 us (3%)
  local copies, waits for them, and re-layouts  4.23 us (2%)
    pallas_call x1, Pallas kernels, exchange(): pl.pallas_call(functools.partial(exchange_kernel, width, depth, split), i...  77.9 us
    all_gather x1, waiting for transfers between devices, per_device(): full = lax.all_gather(col_warped, 'row', axis=1, tiled=True)  49 us
    pallas_call x1, Pallas kernels, match(): pl.pallas_call(functools.partial(match_kernel, reach, offsets), grid=(ima...  18 us
    pallas_call x1, Pallas kernels, subtract(): pl.pallas_call(functools.partial(subtract_kernel, tiles), grid_spec=pltpu...  6.46 us
    dot_general x1, matrix products, per_device(): jnp.einsum('nbs,nst->nbt', images.reshape(count, band, cols), warp_cols.r...  4.71 us
    ppermute x1, starting transfers between devices, per_device(): before = lax.ppermute(rows[:, band - HALO:], 'row', up)  4.04 us
  transfers between devices with their start and end apart: 3, of which 2 were waited for; matrix products, arithmetic and copies ran while one was open for 5% of the time, Pallas kernels for 0%

profile of v2, /device:TPU:1, one launch (start us, length us, event | category | flops | bytes accessed | tf_op | source)
XLA Modules:
  0.0 189.0 jit_solution(12284956181623004109)
XLA Ops:
  7.2 1.3 copy-done
  8.5 4.7 %convolution_convert_fusion = bf16[18,96,384]{2,1,0:T(8,128)(2,1)} fusion(bf16[18,96,384]{2,1,0:T(8,128)(2,1)S(1)} %bitcast.22, bf16[18,384,384]{2,1,0:T(8,128)(2,1)} %bitcast.26), kind=kOutput, calls=%fused_computation.1 | convolution fusion | flops 510271488 | bytes 7962624 | tf_op jit(solution)/shard_map/nbs,nst->nbt/dot_general | solution.py:494
  13.3 1.1 fusion.23
  14.4 4.0 %collective-permute-start = (bf16[18,16,384]{2,1,0:T(8,128)(2,1)S(1)}, bf16[18,16,384]{2,1,0:T(8,128)(2,1)S(1)}, u32[]{:S(2)}, u32[]{:S(2)}) collective-permute-start(bf16[18,16,384]{2,1,0:T(8,128)(2,1)S(1)} %get-tuple-element.9), channel_id=1, source_target_pairs={{0,1},{1,2},{2,3},{4,5},{5,6},{6,7},{8,9},{9,10},{10,11},{12,13},{... | collective-permute-start | bytes 663560 | tf_op jit(solution)/shard_map/ppermute | solution.py:491
  18.5 1.3 collective-permute-start.1
  20.0 0.2 eq.111
  20.4 0.2 broadcast_in_dim.74
  20.6 0.3 broadcast_in_dim.75
  21.1 0.6 fusion.19
  21.7 0.7 compare_reduce_fusion
  22.4 0.7 select_reduce_fusion.4
  23.1 2.0 %pad_maximum_fusion.1.total_ref = f32[3]{0:T(128)S(1)} fusion(f32[1]{0:T(128)} %bitcast.10, f32[1]{0:T(128)} %bitcast.9, f32[1]{0:T(128)} %bitcast.8), kind=kLoop, calls=%fused_computation.41 | loop fusion | flops 6 | bytes 24 | tf_op jit(solution)/shard_map/stack | solution.py:519
  25.1 0.2 select_reduce_fusion.1
  25.3 0.2 fusion
  25.4 0.2 fusion.1
  25.7 0.3 fusion.5.base_ref
  26.0 0.4 collective-permute-done.1
  26.4 1.7 pad_maximum_fusion.rows_ref
  28.2 49.0 %all-gather.2.cloned.1.call-done.full_ref = bf16[18,384,384]{2,1,0:T(8,128)(2,1)} async-done(((bf16[18,96,384]{2,1,0:T(8,128)(2,1)}), bf16[18,384,384]{2,1,0:T(8,128)(2,1)}) %all-gather.2.cloned.1.call-update) | async-done | bytes 5308432 | tf_op jit(solution)/shard_map/all_gather | solution.py:500
  77.2 18.0 %match.1.matched_ref = f32[18,3,96,128]{3,2,1,0:T(8,128)S(1)} custom-call(f32[18,22,128]{2,1,0:T(8,128)S(1)} %fusion.5.base_ref, bf16[18,128,384]{2,1,0:T(8,128)(2,1)S(1)} %pad_maximum_fusion.rows_ref, bf16[18,384,384]{2,1,0:T(8,128)(2,1)} %all-gather.2.cloned.1.call-done.full_ref), custom_call_target="tpu_custom_call" | custom-call | tf_op jit(solution)/shard_map/match/pallas_call | solution.py:74
  95.2 2.0 %collect.1 = bf16[192,96,128]{2,1,0:T(8,128)(2,1)S(1)} custom-call(s32[54]{0:T(128)S(1)} %dynamic-slice_add_fusion.target_ref, f32[18]{0:T(128)S(1)} %dynamic_slice.11.weight_ref, f32[18,3,96,128]{3,2,1,0:T(8,128)S(1)} %match.1.matched_ref), custom_call_target="tpu_custom_call" | custom-call | tf_op jit(solution)/shard_map/collect/pallas_call | solution.py:110
  97.1 77.9 %exchange.1 = (bf16[4,8,2,288,128]{4,3,2,1,0:T(8,128)(2,1)S(1)}, bf16[96,384]{1,0:T(8,128)(2,1)S(1)}) custom-call(f32[3]{0:T(128)S(1)} %pad_maximum_fusion.1.total_ref, bf16[4,8,2,288,128]{4,3,2,1,0:T(8,128)(2,1)S(1)} %bitcast.23), custom_call_target="tpu_custom_call" | custom-call | tf_op jit(solution)/shard_map/exchange/pallas_call | solution.py:424
  175.0 6.5 %subtract.1 = bf16[18,96,384]{2,1,0:T(8,128)(2,1)} custom-call(s32[54]{0:T(128)S(1)} %dynamic-slice_add_fusion.target_ref, f32[18,3,96,128]{3,2,1,0:T(8,128)S(1)} %match.1.matched_ref, bf16[192,96,128]{2,1,0:T(8,128)(2,1)S(1)} %bitcast.24), custom_call_target="tpu_custom_call" | custom-call | tf_op jit(solution)/shard_map/subtract/pallas_call | solution.py:134
  181.5 0.6 copy.18
  (28 shorter events, 0.7 us)
Async XLA Ops:
  7.2 1.3 copy-start
  7.2 70.0 %all-gather.2.cloned.1.call-start = ((), (), s32[]{:S(2)}) async-start(), calls=%async_computation | async-start | bytes 6635520 | tf_op jit(solution)/shard_map/all_gather | solution.py:500
  13.2 6.6 %copy-start.3 = (f32[6,3,21]{2,1,0:T(4,128)S(1)}, f32[6,3,21]{2,1,0:T(4,128)}, u32[]{:S(2)}) copy-start(f32[6,3,21]{2,1,0:T(4,128)} %param.13) | copy-start | bytes 4540
  13.2 6.6 %copy-start.4 = (f32[21,21]{1,0:T(8,128)S(1)}, f32[21,21]{1,0:T(8,128)}, u32[]{:S(2)}) copy-start(f32[21,21]{1,0:T(8,128)} %param.14) | copy-start | bytes 5296
  13.2 6.7 %copy-start.5 = (s32[384,3]{0,1:T(4,128)S(1)}, s32[384,3]{0,1:T(4,128)}, u32[]{:S(2)}) copy-start(s32[384,3]{0,1:T(4,128)} %param.17) | copy-start | bytes 13828
  13.2 7.0 %copy-start.6 = (f32[8]{0:T(128)S(1)}, f32[8]{0:T(128)}, u32[]{:S(2)}) copy-start(f32[8]{0:T(128)} %param.18) | copy-start | bytes 100
  13.2 7.8 %copy-start.2 = (s32[3456,1]{0,1:T(1,128)S(1)}, s32[3456,1]{0,1:T(1,128)}, u32[]{:S(2)}) copy-start(s32[3456,1]{0,1:T(1,128)} %param.15) | copy-start | bytes 41476
  13.2 7.9 %copy-start.7 = (s32[64]{0:T(128)S(1)}, s32[64]{0:T(128)}, u32[]{:S(2)}) copy-start(s32[64]{0:T(128)} %param.19) | copy-start | bytes 772
  13.2 9.2 %copy-start.1 = (s32[3456]{0:T(1024)S(1)}, s32[3456]{0:T(1024)}, u32[]{:S(2)}) copy-start(s32[3456]{0:T(1024)} %param.16) | copy-start | bytes 41476
  14.4 11.6 %collective-permute-start = (bf16[18,16,384]{2,1,0:T(8,128)(2,1)S(1)}, bf16[18,16,384]{2,1,0:T(8,128)(2,1)S(1)}, u32[]{:S(2)}, u32[]{:S(2)}) collective-permute-start(bf16[18,16,384]{2,1,0:T(8,128)(2,1)S(1)} %get-tuple-element.9), channel_id=1, source_target_pairs={{0,1},{1,2},{2,3},{4,5},{5,6},{6,7},{8,9},{9,10},{10,11},{12,13},{... | collective-permute-start | bytes 663560 | tf_op jit(solution)/shard_map/ppermute | solution.py:491
  18.5 8.0 %collective-permute-start.1 = (bf16[18,16,384]{2,1,0:T(8,128)(2,1)S(1)}, bf16[18,16,384]{2,1,0:T(8,128)(2,1)}, u32[]{:S(2)}, u32[]{:S(2)}) collective-permute-start(bf16[18,16,384]{2,1,0:T(8,128)(2,1)S(1)} %get-tuple-element.10), channel_id=1, source_target_pairs={{1,0},{2,1},{3,2},{5,4},{6,5},{7,6},{9,8},{10,9},{11,10},{13,12},{... | collective-permute-start | bytes 663560 | tf_op jit(solution)/shard_map/ppermute | solution.py:492
Sparse Core Ops, SparseCore 0:
  13.4 63.7 all-gather.1

commit v3 on v2

--- a/solution.py
+++ b/solution.py
@@ -13,6 +13,8 @@
 GROUP = 4
 DEPTH = 8
 SPLIT = 128
+PASS_ON = 2
+LAG = 4
 
 
 def build_table(base_ref, image, keep, table_ref, offsets):
@@ -57,40 +59,6 @@
             out_ref[image, tile, pl.ds(2 * pair + 1, groups, stride=GROUP), :] = lower
 
 
-def match_kernel(reach, offsets, base_ref, rows_ref, full_ref, out_ref, window_ref, left_ref, table_ref):
-    @pl.when(pl.program_id(0) == 0)
-    def _():
-        table_ref[...] = jnp.zeros_like(table_ref)
-
-    build_table(base_ref, 0, table_mask(2 * reach + 1), table_ref, offsets)
-    warped = jnp.dot(rows_ref[0], full_ref[0], preferred_element_type=jnp.float32)
-    convolve(warped, reach, window_ref, left_ref, table_ref, out_ref, 0, offsets)
-
-
-def match(base, rows_ext, full, reach):
-    images, ext, cols = rows_ext.shape
-    band = ext - 2 * HALO
-    offsets = 2 * reach + GROUP
-    return pl.pallas_call(
-        functools.partial(match_kernel, reach, offsets),
-        grid=(images,),
-        in_specs=[
-            pl.BlockSpec((1,) + base.shape[1:], lambda i: (i, 0, 0)),
-            pl.BlockSpec((1, ext, cols), lambda i: (i, 0, 0)),
-            pl.BlockSpec((1, cols, cols), lambda i: (i, 0, 0)),
-        ],
-        out_specs=pl.BlockSpec((1, cols // TILE, band, TILE), lambda i: (i, 0, 0, 0)),
-        out_shape=jax.ShapeDtypeStruct((images, cols // TILE, band, TILE), jnp.float32),
-        scratch_shapes=[
-            pltpu.VMEM((2 * (cols // TILE), ext, TILE), jnp.float32),
-            pltpu.VMEM((2 * (cols // TILE) * (band // GROUP), offsets * TILE), jnp.bfloat16),
-            pltpu.VMEM((offsets * TILE, 2 * TILE), jnp.bfloat16),
-        ],
-        compiler_params=pltpu.CompilerParams(vmem_limit_bytes=48 << 20),
-        name="match",
-    )(base, rows_ext, full)
-
-
 def collect_kernel(tiles, target_ref, weight_ref, matched_ref, dense_ref):
     image = pl.program_id(0)
 
@@ -99,7 +67,7 @@
         dense_ref[...] = jnp.zeros_like(dense_ref)
 
     for tile in range(tiles):
-        piece = weight_ref[image] * matched_ref[0, tile]
+        piece = weight_ref[image] * matched_ref[image, tile]
         piece = piece.astype(jnp.bfloat16).astype(jnp.float32)
         target = target_ref[image * tiles + tile]
         dense_ref[target] = (dense_ref[target].astype(jnp.float32) + piece).astype(jnp.bfloat16)
@@ -112,7 +80,7 @@
         grid_spec=pltpu.PrefetchScalarGridSpec(
             num_scalar_prefetch=2,
             grid=(images,),
-            in_specs=[pl.BlockSpec((1, tiles, band, TILE), lambda i, *_: (i, 0, 0, 0))],
+            in_specs=[pl.BlockSpec(memory_space=pltpu.VMEM)],
             out_specs=pl.BlockSpec((boxes, band, TILE), lambda i, *_: (0, 0, 0), pipeline_mode=pl.Buffered(1)),
         ),
         out_shape=jax.ShapeDtypeStruct((boxes, band, TILE), jnp.bfloat16),
@@ -126,7 +94,7 @@
     for tile in range(tiles):
         target = target_ref[image * tiles + tile]
         lanes = pl.ds(tile * TILE, TILE)
-        out_ref[0, :, lanes] = (matched_ref[0, tile] - template_ref[target].astype(jnp.float32)).astype(jnp.bfloat16)
+        out_ref[0, :, lanes] = (matched_ref[image, tile] - template_ref[target].astype(jnp.float32)).astype(jnp.bfloat16)
 
 
 def subtract(targets, matched, templates):
@@ -137,8 +105,8 @@
             num_scalar_prefetch=1,
             grid=(images,),
             in_specs=[
-                pl.BlockSpec((1, tiles, band, TILE), lambda i, *_: (i, 0, 0, 0)),
-                pl.BlockSpec(templates.shape, lambda i, *_: (0, 0, 0), pipeline_mode=pl.Buffered(1)),
+                pl.BlockSpec(memory_space=pltpu.VMEM),
+                pl.BlockSpec(memory_space=pltpu.VMEM),
             ],
             out_specs=pl.BlockSpec((1, band, tiles * TILE), lambda i, *_: (i, 0, 0)),
         ),
@@ -442,6 +410,145 @@
     )(totals, dense)
 
 
+def gather_match_kernel(
+    reach,
+    offsets,
+    base_ref,
+    images_hbm,
+    rows_hbm,
+    cols_hbm,
+    out_ref,
+    images_ref,
+    rows_ref,
+    cols_ref,
+    full_ref,
+    halo_ref,
+    window_ref,
+    left_ref,
+    table_ref,
+    load_ref,
+    send_ref,
+    recv_ref,
+):
+    count, band, side = images_hbm.shape
+    half = band // 2
+    size = full_ref.shape[1]
+    me = lax.axis_index("row")
+    beside = [signed(me, 1, way, size) for way in (0, 1)]
+
+    def local(kind, image):
+        source, target = ((images_hbm, images_ref), (cols_hbm, cols_ref), (rows_hbm, rows_ref))[kind]
+        return pltpu.make_async_copy(source.at[image], target.at[image], load_ref.at[kind, image])
+
+    def remote(kind, image, source, target, way):
+        return pltpu.make_async_remote_copy(
+            src_ref=source,
+            dst_ref=target,
+            send_sem=send_ref.at[kind, image],
+            recv_sem=recv_ref.at[kind, image],
+            device_id={"row": beside[way]},
+            device_id_type=pl.DeviceIdType.MESH,
+        )
+
+    def own(image, way):
+        place = full_ref.at[image, me]
+        return remote(way, image, place, place, way)
+
+    def forward(image, way):
+        place = full_ref.at[image, beside[1 - way], pl.ds(way * half, half), :]
+        return remote(2 + way, image, place, place, way)
+
+    def edge(image, way):
+        start = band - HALO if way == 0 else 0
+        return remote(4 + way, image, rows_hbm.at[image, pl.ds(start, HALO), :], halo_ref.at[image, way], way)
+
+    for kind in range(3):
+        @pl.loop(0, count)
+        def _(image):
+            local(kind, image).start()
+
+    barrier = pltpu.get_barrier_semaphore()
+    for friend in beside:
+        pl.semaphore_signal(barrier, inc=1, device_id={"row": friend}, device_id_type=pl.DeviceIdType.MESH)
+    table_ref[...] = jnp.zeros_like(table_ref)
+    keep = table_mask(2 * reach + 1)
+    first = jnp.where(me == 0, 0.0, 1.0)
+    last = jnp.where(me == size - 1, 0.0, 1.0)
+    pl.semaphore_wait(barrier, 2)
+
+    @pl.loop(0, count + LAG)
+    def _(step):
+        @pl.when(step < count)
+        def _():
+            local(0, step).wait()
+            local(1, step).wait()
+            mapped = jnp.dot(images_ref[step], cols_ref[step], preferred_element_type=jnp.float32)
+            full_ref[step, me] = mapped.astype(jnp.bfloat16)
+            for way in (0, 1):
+                own(step, way).start()
+                edge(step, way).start()
+
+        @pl.when((step >= PASS_ON) & (step < count + PASS_ON))
+        def _():
+            image = step - PASS_ON
+            for way in (0, 1):
+                own(image, way).wait_recv()
+                forward(image, way).start()
+
+        @pl.when(step >= LAG)
+        def _():
+            image = step - LAG
+            build_table(base_ref, image, keep, table_ref, offsets)
+            local(2, image).wait()
+            for way in (0, 1):
+                forward(image, way).wait_recv()
+                edge(image, way).wait_recv()
+            rows = jnp.concatenate([halo_ref[image, 0], rows_ref[image], halo_ref[image, 1]], axis=0)
+            full = full_ref[image].reshape(side, side)
+            warped = jnp.dot(rows, full, preferred_element_type=jnp.float32)
+            warped = jnp.concatenate(
+                [warped[:HALO] * first, warped[HALO : HALO + band], warped[HALO + band :] * last], axis=0
+            )
+            convolve(warped, reach, window_ref, left_ref, table_ref, out_ref, image, offsets)
+
+    @pl.loop(0, count)
+    def _(image):
+        for way in (0, 1):
+            own(image, way).wait_send()
+            forward(image, way).wait_send()
+            edge(image, way).wait_send()
+
+
+def gather_match(base, images, rows, cols, size, reach):
+    count, band, side = images.shape
+    offsets = 2 * reach + GROUP
+    tiles = side // TILE
+    hbm = pl.BlockSpec(memory_space=pl.ANY)
+    return pl.pallas_call(
+        functools.partial(gather_match_kernel, reach, offsets),
+        in_specs=[pl.BlockSpec(memory_space=pltpu.VMEM), hbm, hbm, hbm],
+        out_specs=pl.BlockSpec(memory_space=pltpu.VMEM),
+        out_shape=jax.ShapeDtypeStruct((count, tiles, band, TILE), jnp.float32),
+        scratch_shapes=[
+            pltpu.VMEM((count, band, side), jnp.bfloat16),
+            pltpu.VMEM((count, band, side), jnp.bfloat16),
+            pltpu.VMEM((count, side, side), jnp.bfloat16),
+            pltpu.VMEM((count, size, band, side), jnp.bfloat16),
+            pltpu.VMEM((count, 2, HALO, side), jnp.bfloat16),
+            pltpu.VMEM((2 * tiles, band + 2 * HALO, TILE), jnp.float32),
+            pltpu.VMEM((2 * tiles * (band // GROUP), offsets * TILE), jnp.bfloat16),
+            pltpu.VMEM((offsets * TILE, 2 * TILE), jnp.bfloat16),
+            pltpu.SemaphoreType.DMA((3, count)),
+            pltpu.SemaphoreType.DMA((6, count)),
+            pltpu.SemaphoreType.DMA((6, count)),
+        ],
+        compiler_params=pltpu.CompilerParams(
+            collective_id=1, has_side_effects=True, vmem_limit_bytes=40 << 20
+        ),
+        name="gather_match",
+    )(base, images, rows, cols)
+
+
 def base_rows(psf_coef, taps):
     images = psf_coef.shape[0]
     kernels, span = taps.shape
@@ -485,22 +592,15 @@
     me = lax.axis_index("det")
     row_size = lax.axis_size("row")
 
-    rows = warp_rows.reshape(count, band, cols)
-    up = [(i, i + 1) for i in range(row_size - 1)]
-    down = [(j, i) for i, j in up]
-    before = lax.ppermute(rows[:, band - HALO :], "row", up)
-    after = lax.ppermute(rows[:, :HALO], "row", down)
-    rows_ext = jnp.concatenate([before, rows, after], axis=1)
-    col_warped = jnp.einsum(
-        "nbs,nst->nbt",
+    base = base_rows(psf_coef.reshape(count, -1), taps)
+    matched = gather_match(
+        base,
         images.reshape(count, band, cols),
+        warp_rows.reshape(count, band, cols),
         warp_cols.reshape(count, cols, cols),
-        preferred_element_type=jnp.float32,
-    ).astype(jnp.bfloat16)
-    full = lax.all_gather(col_warped, "row", axis=1, tiled=True)
-
-    base = base_rows(psf_coef.reshape(count, -1), taps)
-    matched = match(base, rows_ext, full, reach)
+        row_size,
+        reach,
+    )
 
     levels = weight_table.shape[0]
     flat_index = weight_index.reshape(-1)

time: 190 us -> 171 us (0.900)
  waiting for transfers between devices: 49.5 us -> 0 us
  Pallas kernels: 104 us -> 151 us
  between operations: 14.2 us -> 0.72 us
  starting transfers between devices: 5.37 us -> 0 us
  local copies, waits for them, and re-layouts: 4.23 us -> 8.39 us
  matrix products: 5.36 us -> 2.07 us
  other arithmetic: 6.07 us -> 8.67 us
    all_gather x1 -> x0, waiting for transfers between devices: 49 us -> none  [per_device(): full = lax.all_gather(col_warped, 'row', axis=1, tiled=True)]
    pallas_call x1, Pallas kernels: 18 us -> 60.7 us  [gather_match(): pl.pallas_call(functools.partial(gather_match_kernel, reach, offsets), in...]
    ppermute x2 -> x0, starting transfers between devices: 5.33 us -> none  [the longest x1 4.04 us: per_device(): before = lax.ppermute(rows[:, band - HALO:], 'row', up)]
    dot_general x1 -> x0, matrix products: 4.71 us -> none  [per_device(): jnp.einsum('nbs,nst->nbt', images.reshape(count, band, cols), warp_cols.r...]
    pallas_call x1, Pallas kernels: 77.9 us -> 81.7 us  [exchange(): pl.pallas_call(functools.partial(exchange_kernel, width, depth, split), i...]
    unnamed x18 -> x8, local copies, waits for them, and re-layouts: 2.08 us -> 5.29 us
  transfers between devices with their start and end apart: 3 -> 0, of which waited for: 2 -> 0; matrix products, arithmetic and copies ran while one was open for 5% -> 0% of each run, Pallas kernels for 0% -> 0%
where the time goes in v3:
time: 171 us
  Pallas kernels  151 us (88%)
  other arithmetic  8.67 us (5%)
  local copies, waits for them, and re-layouts  8.39 us (5%)
  matrix products  2.07 us (1%)
    pallas_call x1, Pallas kernels, exchange(): pl.pallas_call(functools.partial(exchange_kernel, width, depth, split), i...  81.7 us
    pallas_call x1, Pallas kernels, gather_match(): pl.pallas_call(functools.partial(gather_match_kernel, reach, offsets), in...  60.7 us
    pallas_call x1, Pallas kernels, subtract(): pl.pallas_call(functools.partial(subtract_kernel, tiles), grid_spec=pltpu...  6.46 us
    unnamed x8, local copies, waits for them, and re-layouts  5.29 us

profile of v3, /device:TPU:1, one launch (start us, length us, event | category | flops | bytes accessed | tf_op | source)
XLA Modules:
  0.0 170.7 jit_solution(16068847900845996523)
XLA Ops:
  0.6 1.4 fusion.19
  2.0 0.8 dynamic-slice_bitcast_fusion
  2.8 0.8 select_reduce_fusion.1
  3.6 0.8 dynamic-slice_add_fusion.target_ref
  4.4 1.4 compare_reduce_fusion
  5.8 0.9 fusion
  6.7 0.9 fusion.1
  7.6 0.7 mul.36
  8.4 0.8 copy.15
  9.2 0.3 fusion.5.base_ref
  9.4 0.8 copy.16
  10.3 0.2 eq.111
  10.5 0.7 select_reduce_fusion
  11.3 0.2 broadcast_in_dim.74
  11.5 0.3 broadcast_in_dim.75
  11.9 1.4 select_reduce_fusion.4
  13.3 2.1 %pad_maximum_fusion.total_ref = f32[3]{0:T(128)S(1)} fusion(f32[1]{0:T(128)} %bitcast.10, f32[1]{0:T(128)} %bitcast.9, f32[1]{0:T(128)} %bitcast.8), kind=kLoop, calls=%fused_computation.39 | loop fusion | flops 6 | bytes 24 | tf_op jit(solution)/shard_map/stack | solution.py:619
  15.3 2.5 %copy-done = bf16[6,3,384,384]{3,2,1,0:T(8,128)(2,1)S(1)} copy-done((bf16[6,3,384,384]{3,2,1,0:T(8,128)(2,1)S(1)}, bf16[6,3,384,384]{3,2,1,0:T(8,128)(2,1)}, u32[]{:S(2)}) %copy-start) | copy-done | bytes 5308440
  17.9 1.3 copy-done.2
  19.2 60.7 %gather_match.1.matched_ref = f32[18,3,96,128]{3,2,1,0:T(8,128)S(1)} custom-call(f32[18,22,128]{2,1,0:T(8,128)S(1)} %fusion.5.base_ref, bf16[18,96,384]{2,1,0:T(8,128)(2,1)S(1)} %bitcast.23, bf16[18,96,384]{2,1,0:T(8,128)(2,1)S(1)} %bitcast.24, bf16[18,384,384]{2,1,0:T(8,128)(2,1)S(1)} %bitcast.21), custom_call_target="tpu_custom_call" | custom-call | tf_op jit(solution)/shard_map/gather_match/pallas_call | solution.py:527
  79.9 1.9 %collect.1 = bf16[192,96,128]{2,1,0:T(8,128)(2,1)S(1)} custom-call(s32[54]{0:T(128)S(1)} %dynamic-slice_add_fusion.target_ref, f32[18]{0:T(128)S(1)} %dynamic_slice.11.weight_ref, f32[18,3,96,128]{3,2,1,0:T(8,128)S(1)} %gather_match.1.matched_ref), custom_call_target="tpu_custom_call" | custom-call | tf_op jit(solution)/shard_map/collect/pallas_call | solution.py:78
  81.8 81.7 %exchange.1 = (bf16[4,8,2,288,128]{4,3,2,1,0:T(8,128)(2,1)S(1)}, bf16[96,384]{1,0:T(8,128)(2,1)S(1)}) custom-call(f32[3]{0:T(128)S(1)} %pad_maximum_fusion.total_ref, bf16[4,8,2,288,128]{4,3,2,1,0:T(8,128)(2,1)S(1)} %bitcast.20), custom_call_target="tpu_custom_call" | custom-call | tf_op jit(solution)/shard_map/exchange/pallas_call | solution.py:392
  163.6 6.5 %subtract.1 = bf16[18,96,384]{2,1,0:T(8,128)(2,1)} custom-call(s32[54]{0:T(128)S(1)} %dynamic-slice_add_fusion.target_ref, f32[18,3,96,128]{3,2,1,0:T(8,128)S(1)} %gather_match.1.matched_ref, bf16[192,96,128]{2,1,0:T(8,128)(2,1)S(1)} %bitcast.22), custom_call_target="tpu_custom_call" | custom-call | tf_op jit(solution)/shard_map/subtract/pallas_call | solution.py:102
  170.0 0.6 copy.18
  (8 shorter events, 0.1 us)
Async XLA Ops:
  0.6 14.7 %copy-start.1 = (bf16[6,3,96,384]{3,2,1,0:T(8,128)(2,1)S(1)}, bf16[6,3,96,384]{3,2,1,0:T(8,128)(2,1)}, u32[]{:S(2)}) copy-start(bf16[6,3,96,384]{3,2,1,0:T(8,128)(2,1)} %param.10) | copy-start | bytes 3981316
  15.3 2.5 %copy-start = (bf16[6,3,384,384]{3,2,1,0:T(8,128)(2,1)S(1)}, bf16[6,3,384,384]{3,2,1,0:T(8,128)(2,1)}, u32[]{:S(2)}) copy-start(bf16[6,3,384,384]{3,2,1,0:T(8,128)(2,1)} %param.12) | copy-start | bytes 15925252
  17.9 1.3 copy-start.2

commit v4 on v3

--- a/solution.py
+++ b/solution.py
@@ -15,11 +15,81 @@
 SPLIT = 128
 PASS_ON = 2
 LAG = 4
-
-
-def build_table(base_ref, image, keep, table_ref, offsets):
+SUBTRACT_STEPS = 3
+
+
+def one_hot(mask):
+    return jnp.where(mask, 1.0, 0.0).astype(jnp.bfloat16)
+
+
+def iota2(rows, cols, axis):
+    return lax.broadcasted_iota(jnp.int32, (rows, cols), axis)
+
+
+def tap_parts(taps, offsets):
+    kernels, span = taps.shape
+    shift = iota2(offsets, span, 0) - iota2(offsets, span, 1)
+
+    def by_offset(late):
+        pick = jnp.where(shift == late, 1.0, 0.0)
+        return lax.dot_general(
+            pick, taps, (((1,), (1,)), ((), ())), precision=lax.Precision.HIGHEST, preferred_element_type=jnp.float32
+        )
+
+    tap, lane = iota2(span, TILE, 0), iota2(span, TILE, 1)
+    half = taps.astype(jnp.bfloat16)
+
+    def placed(mask):
+        return jnp.dot(half, one_hot(mask), preferred_element_type=jnp.float32).astype(jnp.bfloat16)
+
+    here = placed((lane + tap == TILE) | ((tap == 0) & (lane == 0)))
+    there = placed(lane + tap == HALF)
+    return by_offset(0), by_offset(1), here, there
+
+
+def base_rows(coef, parts):
+    lead, late, here, there = parts
+    left = jnp.dot((coef * lead).astype(jnp.bfloat16), here, preferred_element_type=jnp.float32)
+    return left + jnp.dot((coef * late).astype(jnp.bfloat16), there, preferred_element_type=jnp.float32)
+
+
+def denominators(patch_ref, block_ref, index_ref, table_ref, home_ref, out_ref, boxes):
+    me = lax.axis_index("det")
+    homes = home_ref[...]
+    mine = jnp.sum(jnp.where(homes == me, iota2(1, homes.shape[1], 1), 0), axis=1, keepdims=True)
+    visits, dets = index_ref.shape
+    groups = dets // TILE
+    period = visits * boxes
+    row, lane = iota2(TILE, TILE, 0), iota2(TILE, TILE, 1)
+    blank = jnp.zeros((8 - groups, TILE), jnp.float32)
+    levels = []
+    for visit in range(visits):
+        parts = [index_ref[pl.ds(visit, 1), pl.ds(g * TILE, TILE)].astype(jnp.float32) for g in range(groups)]
+        levels.append(jnp.concatenate(parts + [blank], axis=0).astype(jnp.bfloat16))
+    sums = [jnp.zeros((groups, TILE), jnp.float32) for _ in range(boxes)]
+    for k in range(period):
+        level = jnp.zeros((8, TILE), jnp.float32)
+        for visit in range(visits):
+            gap = lane - period * row + (TILE * k - boxes * visit)
+            level = level + jnp.dot(
+                levels[visit], one_hot((gap >= 0) & (gap < boxes)), preferred_element_type=jnp.float32
+            )
+        level = level[:groups]
+        weight = jnp.zeros((groups, TILE), jnp.float32)
+        for n in range(table_ref.shape[0]):
+            weight = jnp.where(level == float(n), table_ref[n], weight)
+        patch = jnp.concatenate([patch_ref[pl.ds(g * period + k, 1), :] for g in range(groups)], axis=0)
+        block = jnp.concatenate([block_ref[pl.ds(g * period + k, 1), :] for g in range(groups)], axis=0)
+        for box in range(boxes):
+            sums[box] = sums[box] + jnp.where((patch == mine) & (block == box), weight, 0.0)
+    for box in range(boxes):
+        total = jnp.sum(jnp.sum(sums[box], axis=0, keepdims=True), axis=1, keepdims=True)
+        out_ref[pl.ds(box, 1), :] = jnp.broadcast_to(jnp.maximum(total, 1.0), (1, TILE))
+
+
+def build_table(base, keep, table_ref, offsets):
     for t in range(offsets - 2):
-        row = jnp.broadcast_to(base_ref[image, pl.ds(t, 1), :], keep.shape)
+        row = jnp.broadcast_to(base[t : t + 1], keep.shape)
         band = pltpu.roll(row, 0, 1, stride=1, stride_axis=0)
         band = jnp.where(keep, band, 0.0).astype(jnp.bfloat16)
         table_ref[pl.ds(t * TILE, keep.shape[0]), pl.ds(0, TILE)] = band
@@ -59,61 +129,79 @@
             out_ref[image, tile, pl.ds(2 * pair + 1, groups, stride=GROUP), :] = lower
 
 
-def collect_kernel(tiles, target_ref, weight_ref, matched_ref, dense_ref):
-    image = pl.program_id(0)
-
-    @pl.when(image == 0)
-    def _():
-        dense_ref[...] = jnp.zeros_like(dense_ref)
-
-    for tile in range(tiles):
-        piece = weight_ref[image] * matched_ref[image, tile]
-        piece = piece.astype(jnp.bfloat16).astype(jnp.float32)
-        target = target_ref[image * tiles + tile]
-        dense_ref[target] = (dense_ref[target].astype(jnp.float32) + piece).astype(jnp.bfloat16)
-
-
-def collect(targets, weights, matched, boxes):
+def collect_kernel(count, patch_ref, block_ref, index_ref, levels_ref, home_ref, matched_ref, dense_ref, target_ref):
+    dets, tiles = count
+    visits = index_ref.shape[0]
+    me = lax.axis_index("det")
+    dense_ref[...] = jnp.zeros_like(dense_ref)
+
+    @pl.loop(0, dets)
+    def _(det):
+        for visit in range(visits):
+            weight = levels_ref[index_ref[visit, me * dets + det]]
+            for tile in range(tiles):
+                local = (det * visits + visit) * tiles + tile
+                piece = me * dets * visits * tiles + local
+                row, lane = piece // TILE, lax.rem(piece, TILE)
+                target = home_ref[patch_ref[row, lane]] * tiles + block_ref[row, lane]
+                target_ref[local] = target
+                value = (weight * matched_ref[det * visits + visit, tile]).astype(jnp.bfloat16)
+                held = dense_ref[target].astype(jnp.float32)
+                dense_ref[target] = (held + value.astype(jnp.float32)).astype(jnp.bfloat16)
+
+
+def collect(patch, block, index, levels, home, matched, boxes):
     images, tiles, band, _ = matched.shape
+    smem = pl.BlockSpec(memory_space=pltpu.SMEM)
+    vmem = pl.BlockSpec(memory_space=pltpu.VMEM)
     return pl.pallas_call(
-        functools.partial(collect_kernel, tiles),
-        grid_spec=pltpu.PrefetchScalarGridSpec(
-            num_scalar_prefetch=2,
-            grid=(images,),
-            in_specs=[pl.BlockSpec(memory_space=pltpu.VMEM)],
-            out_specs=pl.BlockSpec((boxes, band, TILE), lambda i, *_: (0, 0, 0), pipeline_mode=pl.Buffered(1)),
-        ),
-        out_shape=jax.ShapeDtypeStruct((boxes, band, TILE), jnp.bfloat16),
+        functools.partial(collect_kernel, (images // index.shape[0], tiles)),
+        in_specs=[smem] * 5 + [vmem],
+        out_specs=[vmem, smem],
+        out_shape=[
+            jax.ShapeDtypeStruct((boxes, band, TILE), jnp.bfloat16),
+            jax.ShapeDtypeStruct((images * tiles,), jnp.int32),
+        ],
         compiler_params=pltpu.CompilerParams(vmem_limit_bytes=32 << 20),
         name="collect",
-    )(targets, weights, matched)
-
-
-def subtract_kernel(tiles, target_ref, matched_ref, template_ref, out_ref):
-    image = pl.program_id(0)
-    for tile in range(tiles):
-        target = target_ref[image * tiles + tile]
-        lanes = pl.ds(tile * TILE, TILE)
-        out_ref[0, :, lanes] = (matched_ref[image, tile] - template_ref[target].astype(jnp.float32)).astype(jnp.bfloat16)
-
-
-def subtract(targets, matched, templates):
+    )(patch, block, index, levels, home, matched)
+
+
+def subtract_kernel(tiles, target_ref, matched_ref, template_ref, coadd_ref, out_ref, coadd_out):
+    step = pl.program_id(0)
+    images = out_ref.shape[0]
+
+    @pl.when(step == 0)
+    def _():
+        coadd_out[...] = coadd_ref[...]
+
+    @pl.loop(0, images)
+    def _(local):
+        image = step * images + local
+        for tile in range(tiles):
+            template = template_ref[target_ref[image * tiles + tile]].astype(jnp.float32)
+            out_ref[local, :, pl.ds(tile * TILE, TILE)] = (matched_ref[image, tile] - template).astype(jnp.bfloat16)
+
+
+def subtract(targets, matched, templates, coadd):
     images, tiles, band, _ = matched.shape
+    steps = SUBTRACT_STEPS
+    vmem = pl.BlockSpec(memory_space=pltpu.VMEM)
     return pl.pallas_call(
         functools.partial(subtract_kernel, tiles),
-        grid_spec=pltpu.PrefetchScalarGridSpec(
-            num_scalar_prefetch=1,
-            grid=(images,),
-            in_specs=[
-                pl.BlockSpec(memory_space=pltpu.VMEM),
-                pl.BlockSpec(memory_space=pltpu.VMEM),
-            ],
-            out_specs=pl.BlockSpec((1, band, tiles * TILE), lambda i, *_: (i, 0, 0)),
-        ),
-        out_shape=jax.ShapeDtypeStruct((images, band, tiles * TILE), jnp.bfloat16),
+        grid=(steps,),
+        in_specs=[pl.BlockSpec(memory_space=pltpu.SMEM), vmem, vmem, vmem],
+        out_specs=[
+            pl.BlockSpec((images // steps, band, tiles * TILE), lambda i: (i, 0, 0)),
+            pl.BlockSpec(coadd.shape, lambda i: (0, 0)),
+        ],
+        out_shape=[
+            jax.ShapeDtypeStruct((images, band, tiles * TILE), jnp.bfloat16),
+            jax.ShapeDtypeStruct(coadd.shape, jnp.bfloat16),
+        ],
         compiler_params=pltpu.CompilerParams(vmem_limit_bytes=32 << 20),
         name="subtract",
-    )(targets, matched, templates)
+    )(targets, matched, templates, coadd)
 
 
 def det_index(x, z, core, depth):
@@ -305,7 +393,7 @@
             while start < end:
                 box = start // band
                 stop = min(end, (box + 1) * band)
-                part = total[start - offset - lo : stop - offset - lo] / jnp.maximum(total_ref[box], 1.0)
+                part = total[start - offset - lo : stop - offset - lo] / total_ref[pl.ds(box, 1), :]
                 part = part.astype(jnp.bfloat16)
                 all_ref[x, z, core, pl.ds(start, stop - start), :] = part
                 coadd_ref[pl.ds(start - box * band, stop - start), pl.ds(box * TILE, TILE)] = part
@@ -377,9 +465,8 @@
     links.finish()
 
 
-def exchange(totals, dense, width, depth, split):
+def exchange(totals, dense, band, width, depth, split):
     rows = dense.shape[3]
-    band = rows // totals.shape[0]
     rest = rows - split
     copies = 2 * (2 * width + 2 * depth + 4) + 16
 
@@ -391,11 +478,11 @@
 
     return pl.pallas_call(
         functools.partial(exchange_kernel, width, depth, split),
-        in_specs=[pl.BlockSpec(memory_space=pltpu.SMEM), pl.BlockSpec(memory_space=pltpu.VMEM)],
+        in_specs=[pl.BlockSpec(memory_space=pltpu.VMEM)] * 2,
         out_specs=[pl.BlockSpec(memory_space=pltpu.VMEM)] * 2,
         out_shape=[
             jax.ShapeDtypeStruct(dense.shape, jnp.bfloat16),
-            jax.ShapeDtypeStruct((band, totals.shape[0] * TILE), jnp.bfloat16),
+            jax.ShapeDtypeStruct((band, rows // band * TILE), jnp.bfloat16),
         ],
         scratch_shapes=[pltpu.VMEM((width, depth, rows, TILE), jnp.bfloat16)]
         + buffers(depth, width, split)
@@ -413,11 +500,18 @@
 def gather_match_kernel(
     reach,
     offsets,
-    base_ref,
+    coef_ref,
+    taps_ref,
+    patch_ref,
+    block_ref,
+    index_ref,
+    levels_ref,
+    home_ref,
     images_hbm,
     rows_hbm,
     cols_hbm,
     out_ref,
+    total_ref,
     images_ref,
     rows_ref,
     cols_ref,
@@ -472,6 +566,8 @@
         pl.semaphore_signal(barrier, inc=1, device_id={"row": friend}, device_id_type=pl.DeviceIdType.MESH)
     table_ref[...] = jnp.zeros_like(table_ref)
     keep = table_mask(2 * reach + 1)
+    parts = tap_parts(taps_ref[...], offsets)
+    visits = coef_ref.shape[1]
     first = jnp.where(me == 0, 0.0, 1.0)
     last = jnp.where(me == size - 1, 0.0, 1.0)
     pl.semaphore_wait(barrier, 2)
@@ -488,6 +584,10 @@
                 own(step, way).start()
                 edge(step, way).start()
 
+        @pl.when(step == PASS_ON - 1)
+        def _():
+            denominators(patch_ref, block_ref, index_ref, levels_ref, home_ref, total_ref, out_ref.shape[1])
+
         @pl.when((step >= PASS_ON) & (step < count + PASS_ON))
         def _():
             image = step - PASS_ON
@@ -498,7 +598,8 @@
         @pl.when(step >= LAG)
         def _():
             image = step - LAG
-            build_table(base_ref, image, keep, table_ref, offsets)
+            coef = coef_ref[image // visits, pl.ds(lax.rem(image, visits), 1), :]
+            build_table(base_rows(coef, parts), keep, table_ref, offsets)
             local(2, image).wait()
             for way in (0, 1):
                 forward(image, way).wait_recv()
@@ -519,16 +620,22 @@
             edge(image, way).wait_send()
 
 
-def gather_match(base, images, rows, cols, size, reach):
+def gather_match(coef, taps, patch, block, index, levels, home, images, rows, cols, size):
     count, band, side = images.shape
+    reach = (taps.shape[1] - 1) // 2
     offsets = 2 * reach + GROUP
     tiles = side // TILE
-    hbm = pl.BlockSpec(memory_space=pl.ANY)
+    hbm = pl.BlockSpec(memory_space=pltpu.MemorySpace.HBM)
+    vmem = pl.BlockSpec(memory_space=pltpu.VMEM)
+    smem = pl.BlockSpec(memory_space=pltpu.SMEM)
     return pl.pallas_call(
         functools.partial(gather_match_kernel, reach, offsets),
-        in_specs=[pl.BlockSpec(memory_space=pltpu.VMEM), hbm, hbm, hbm],
-        out_specs=pl.BlockSpec(memory_space=pltpu.VMEM),
-        out_shape=jax.ShapeDtypeStruct((count, tiles, band, TILE), jnp.float32),
+        in_specs=[vmem, vmem, vmem, vmem, vmem, smem, vmem, hbm, hbm, hbm],
+        out_specs=[vmem, vmem],
+        out_shape=[
+            jax.ShapeDtypeStruct((count, tiles, band, TILE), jnp.float32),
+            jax.ShapeDtypeStruct((8, TILE), jnp.float32),
+        ],
         scratch_shapes=[
             pltpu.VMEM((count, band, side), jnp.bfloat16),
             pltpu.VMEM((count, band, side), jnp.bfloat16),
@@ -543,33 +650,10 @@
             pltpu.SemaphoreType.DMA((6, count)),
         ],
         compiler_params=pltpu.CompilerParams(
-            collective_id=1, has_side_effects=True, vmem_limit_bytes=40 << 20
+            collective_id=1, has_side_effects=True, vmem_limit_bytes=46 << 20
         ),
         name="gather_match",
-    )(base, images, rows, cols)
-
-
-def base_rows(psf_coef, taps):
-    images = psf_coef.shape[0]
-    kernels, span = taps.shape
-    scaled = (psf_coef[:, :, None] * taps[None]).astype(jnp.bfloat16)
-    by_tap = jnp.transpose(scaled, (0, 2, 1))
-    lead = jnp.pad(by_tap, ((0, 0), (0, 1), (0, 0)))
-    late = jnp.pad(by_tap, ((0, 0), (1, 0), (0, 0)))
-    both = jnp.concatenate([lead, late], axis=2)
-    lanes = jnp.arange(TILE)[None, :]
-    taken = jnp.arange(span)[:, None]
-    here = ((-taken) % TILE == lanes).astype(jnp.float32)
-    there = (HALF - taken == lanes).astype(jnp.float32)
-    half = taps.astype(jnp.bfloat16).astype(jnp.float32)
-    placed = jnp.concatenate(
-        [
-            jnp.dot(half, here, precision=lax.Precision.HIGHEST),
-            jnp.dot(half, there, precision=lax.Precision.HIGHEST),
-        ],
-        axis=0,
-    ).astype(jnp.bfloat16)
-    return jnp.einsum("itk,kc->itc", both, placed, preferred_element_type=jnp.float32)
+    )(coef, taps, patch, block, index, levels, home, images, rows, cols)
 
 
 def per_device(
@@ -585,48 +669,33 @@
     patch_home,
 ):
     dets, visits, band, cols = images.shape
-    reach = (taps.shape[1] - 1) // 2
     tiles = cols // TILE
     count = dets * visits
     patches = patch_home.shape[0]
-    me = lax.axis_index("det")
     row_size = lax.axis_size("row")
-
-    base = base_rows(psf_coef.reshape(count, -1), taps)
-    matched = gather_match(
-        base,
+    patch = dest_patch.reshape(-1, TILE)
+    block = dest_block.reshape(-1, TILE)
+    index = weight_index.T
+
+    matched, totals = gather_match(
+        psf_coef,
+        taps,
+        patch,
+        block,
+        index,
+        weight_table,
+        patch_home[None],
         images.reshape(count, band, cols),
         warp_rows.reshape(count, band, cols),
         warp_cols.reshape(count, cols, cols),
         row_size,
-        reach,
-    )
-
-    levels = weight_table.shape[0]
-    flat_index = weight_index.reshape(-1)
-    weight_all = jnp.sum(
-        jnp.where(flat_index[:, None] == jnp.arange(levels)[None, :], weight_table[None, :], 0.0), axis=1
-    )
-    weight_mine = lax.dynamic_slice_in_dim(weight_all, me * count, count, 0)
-    patch_mine = lax.dynamic_slice_in_dim(dest_patch[:, 0], me * count * tiles, count * tiles, 0)
-    block_mine = lax.dynamic_slice_in_dim(dest_block, me * count * tiles, count * tiles, 0)
-    home_mine = jnp.sum(
-        jnp.where(patch_mine[:, None] == jnp.arange(patches)[None, :], patch_home[None, :], 0), axis=1
-    )
-    targets = home_mine * tiles + block_mine
-    my_patch = jnp.sum(jnp.where(patch_home == me, jnp.arange(patches), 0))
-    to_mine = jnp.where(dest_patch[:, 0] == my_patch, dest_block, -1).reshape(-1, tiles)
-    denominator = jnp.stack(
-        [jnp.sum(jnp.where(to_mine == b, weight_all[:, None], 0.0)) for b in range(tiles)]
-    )
-
-    dense = collect(targets, weight_mine, matched, patches * tiles)
+    )
+    dense, targets = collect(patch, block, index, weight_table, patch_home, matched, patches * tiles)
     depth = DEPTH
     width = patches // (2 * depth)
     shape = (width, depth, 2, tiles * band, TILE)
-    templates, coadd = exchange(denominator, dense.reshape(shape), width, depth, SPLIT)
-    templates = templates.reshape(patches * tiles, band, TILE)
-    difference = subtract(targets, matched, templates)
+    templates, coadd = exchange(totals, dense.reshape(shape), band, width, depth, SPLIT)
+    difference, coadd = subtract(targets, matched, templates.reshape(patches * tiles, band, TILE), coadd)
     return (difference.reshape(dets, visits, band, cols), coadd[None])
 
 

time: 171 us -> 156 us (0.912)
  other arithmetic: 8.67 us -> 0.75 us
  Pallas kernels: 151 us -> 147 us
  matrix products: 2.07 us -> 0 us
    reduce_sum x4 -> x0, other arithmetic: 4.39 us -> none  [the longest x1 1.42 us: per_device(): jnp.sum(jnp.where(to_mine == b, weight_all[:, None], 0.0))]
    pallas_call x2, Pallas kernels: 8.41 us -> 5.41 us  [the longest x1 2.99 us: collect(): pl.pallas_call(functools.partial(collect_kernel, (images // index.shape[0...]
    dot_general x3 -> x0, matrix products: 2.07 us -> none  [the longest x1 0.9 us: base_rows(): jnp.dot(half, here, precision=lax.Precision.HIGHEST)]
    another operation x1 -> x0, other arithmetic: 2.05 us -> none  [per_device(): jnp.stack([jnp.sum(jnp.where(to_mine == b, weight_all[:, None], 0.0)) for...]
    unnamed x8 -> x16, local copies, waits for them, and re-layouts: 5.29 us -> 6.77 us
where the time goes in v4:
time: 156 us; the launch traced here: 155 us
  Pallas kernels  147 us (94%)
  local copies, waits for them, and re-layouts  6.77 us (4%)
    pallas_call x1, Pallas kernels, exchange(): pl.pallas_call(functools.partial(exchange_kernel, width, depth, split), i...  81.2 us
    pallas_call x1, Pallas kernels, gather_match(): pl.pallas_call(functools.partial(gather_match_kernel, reach, offsets), in...  60.2 us
    unnamed x16, local copies, waits for them, and re-layouts  6.77 us

profile of v4, /device:TPU:1, one launch (start us, length us, event | category | flops | bytes accessed | tf_op | source)
XLA Modules:
  0.0 155.0 jit_solution(5332733318273254799)
XLA Ops:
  0.6 0.8 reduce
  1.4 0.0 copy-start
  1.4 1.3 copy-done
  2.7 0.0 copy-start.1
  2.7 1.3 copy-done.1
  4.0 0.0 copy-start.2
  4.0 0.7 copy-done.2
  4.7 0.0 copy-start.3
  4.8 0.7 copy-done.3
  5.4 0.0 copy-start.4
  5.4 0.7 copy-done.4
  6.1 0.0 copy-start.5
  6.2 0.7 copy-done.5
  6.9 0.0 copy-start.6
  6.9 0.7 copy-done.6
  7.5 0.0 copy-start.7
  7.5 0.7 copy-done.7
  8.2 60.2 %gather_match.1 = (f32[18,3,96,128]{3,2,1,0:T(8,128)S(1)}, f32[8,128]{1,0:T(8,128)S(1)}) custom-call(f32[6,3,21]{2,1,0:T(4,128)S(1)} %copy-done.4, f32[21,21]{1,0:T(8,128)S(1)} %copy-done.5, s32[27,128]{1,0:T(8,128)S(1)} %bitcast.15, s32[27,128]{1,0:T(8,128)S(1)} %bitcast.17, s32[3,384]{1,0:T(4,128)S(1)} %bitcast.19, f32[8]{0:T(128)S(1)} %copy-done.6, ...), custom_call_target="tpu_custom_call" | custom-call | tf_op jit(solution)/shard_map/gather_match/pallas_call | solution.py:631
  68.4 3.0 %collect.1 = (bf16[192,96,128]{2,1,0:T(8,128)(2,1)S(1)}, s32[54]{0:T(128)S(1)}) custom-call(s32[27,128]{1,0:T(8,128)S(1)} %bitcast.16, s32[27,128]{1,0:T(8,128)S(1)} %bitcast.18, s32[3,384]{1,0:T(4,128)S(1)} %bitcast.20, f32[8]{0:T(128)S(1)} %copy-done.6, s32[64]{0:T(128)S(1)} %copy-done.7, f32[18,3,96,128]{3,2,1,0:T(8,128)S(1)} %get-tuple-element.10.matched_ref), custom_call_target="tpu_custom_call" | custom-call | tf_op jit(solution)/shard_map/collect/pallas_call | solution.py:157
  71.4 81.2 %exchange.1 = (bf16[4,8,2,288,128]{4,3,2,1,0:T(8,128)(2,1)S(1)}, bf16[96,384]{1,0:T(8,128)(2,1)S(1)}) custom-call(f32[8,128]{1,0:T(8,128)S(1)} %get-tuple-element.12.total_ref, bf16[4,8,2,288,128]{4,3,2,1,0:T(8,128)(2,1)S(1)} %bitcast.12), custom_call_target="tpu_custom_call" | custom-call | tf_op jit(solution)/shard_map/exchange/pallas_call | solution.py:479
  152.6 2.4 %subtract.1 = (bf16[18,96,384]{2,1,0:T(8,128)(2,1)}, bf16[96,384]{1,0:T(8,128)(2,1)}) custom-call(s32[54]{0:T(128)S(1)} %get-tuple-element.11.target_ref, f32[18,3,96,128]{3,2,1,0:T(8,128)S(1)} %get-tuple-element.10.matched_ref, bf16[192,96,128]{2,1,0:T(8,128)(2,1)S(1)} %bitcast.11, bf16[96,384]{1,0:T(8,128)(2,1)S(1)} %get-tuple-element.15.coadd_ref), custom_call_target="tpu_custom_call" | custom-call | tf_op jit(solution)/shard_map/subtract/pallas_call | solution.py:190
Async XLA Ops:
  1.4 1.3 copy-start
  2.7 1.3 copy-start.1
  4.0 0.7 copy-start.2
  4.7 0.7 copy-start.3
  5.4 0.7 copy-start.4
  6.1 0.7 copy-start.5
  6.9 0.7 copy-start.6
  7.5 0.7 copy-start.7

commit v5 on v4

--- a/solution.py
+++ b/solution.py
@@ -12,7 +12,8 @@
 HALO = 16
 GROUP = 4
 DEPTH = 8
-SPLIT = 128
+STREAMS = (("a", "z", 0, 64), ("c", "z", 64, 64), ("b", "x", 128, 96), ("d", "x", 224, 64))
+ORDER = "bcdacbaacdbbabddcaabdaccbdaacbbdabccddabacdbccdbbadcaddcbcadbacd"
 PASS_ON = 2
 LAG = 4
 SUBTRACT_STEPS = 3
@@ -306,190 +307,145 @@
     yield
 
 
-def exchange_kernel(
-    width,
-    depth,
-    split,
-    total_ref,
-    dense_ref,
-    all_ref,
-    coadd_ref,
-    held_ref,
-    az_ref,
-    az_half,
-    ax_ref,
-    ax_half,
-    bx_ref,
-    bx_half,
-    bz_ref,
-    bz_half,
-    send_ref,
-    recv_ref,
-):
-    rows = dense_ref.shape[3]
+def chunk_order(size):
+    middle = size // 2
+    return [[(middle, 0)]] + [[(step, 0), (step, 1)] for step in range(middle - 1, 0, -1)] + [[(0, 0)]]
+
+
+def exchange_kernel(width, depth, total_ref, dense_ref, all_ref, coadd_ref, held_ref, send_ref, recv_ref, *buffers):
     band = coadd_ref.shape[0]
     me = lax.axis_index("det")
     core = lax.rem(me, 2)
     z = lax.rem(me // 2, depth)
     x = me // (2 * depth)
     other = {"det": det_index(x, z, 1 - core, depth)}
-    beside = [{"det": det_index(signed(x, 1, way, width), z, core, depth)} for way in (0, 1)]
-    along = [{"det": det_index(x, signed(z, 1, way, depth), core, depth)} for way in (0, 1)]
+    ways = {
+        "x": [{"det": det_index(signed(x, 1, way, width), z, core, depth)} for way in (0, 1)],
+        "z": [{"det": det_index(x, signed(z, 1, way, depth), core, depth)} for way in (0, 1)],
+    }
+    sizes, places = {"x": width, "z": depth}, {"x": x, "z": z}
     barrier = pltpu.get_barrier_semaphore()
-    friends = [other] + beside + along
+    friends = [other] + ways["x"] + ways["z"]
     for friend in friends:
         pl.semaphore_signal(barrier, inc=1, device_id=friend, device_id_type=pl.DeviceIdType.MESH)
     pl.semaphore_wait(barrier, len(friends))
-
     links = Links(send_ref, recv_ref)
-    rest = rows - split
-
-    def everything(l, size):
-        return pl.ds(0, size) if l is None else l
-
-    def a_at(dest, l, lo, length):
-        return (everything(l, width), dest, pl.ds(lo, length), slice(None))
-
-    def b_at(dest, l, lo, length):
-        return (dest, everything(l, depth), pl.ds(split + lo, length), slice(None))
-
-    def a_next(dest, l, lo, length):
-        return (pl.ds(dest, 1) if l is None else dest, z, pl.ds(lo, length), slice(None))
-
-    def b_next(dest, l, lo, length):
-        return (pl.ds(x, 1) if l is None else x, dest, pl.ds(split + lo, length), slice(None))
 
     def with_core(index, which):
         return index[:2] + (which,) + index[2:]
 
-    def hand_over(tag, dest, at, length):
-        index = at(dest, None, 0, length)
-        links.start(tag, dense_ref.at[with_core(index, 1 - core)], held_ref.at[index], other)
-
-    zs = [(depth // 2, 0)] + [(s, w) for s in range(depth // 2 - 1, 0, -1) for w in (0, 1)] + [(0, 0)]
-    xs = [(width // 2, 0)] + [(s, w) for s in range(width // 2 - 1, 0, -1) for w in (0, 1)] + [(0, 0)]
-    turns = [("b", xs[0]), ("a", zs[0]), ("a", zs[1]), ("a", zs[2])]
-    turns += [("b", k) for k in xs[1:-1]] + [("a", k) for k in zs[3:]] + [("b", xs[-1])]
-    for part, (step, way) in turns:
-        if part == "a":
-            hand_over(("core a", step, way), signed(z, step, way, depth), a_at, split)
-        else:
-            hand_over(("core b", step, way), signed(x, step, way, width), b_at, rest)
-
-    def base_of(tag, order, at):
-        left = list(order)
+    def indices(first, start):
+        second = "x" if first == "z" else "z"
+
+        def order(dest, across):
+            return (across, dest) if first == "z" else (dest, across)
+
+        def wide(dest, l, lo, length):
+            across = pl.ds(0, sizes[second]) if l is None else l
+            return order(dest, across) + (pl.ds(start + lo, length), slice(None))
+
+        def narrow(dest, l, lo, length):
+            across = pl.ds(places[first], 1) if l is None else places[first]
+            return order(across, dest) + (pl.ds(start + lo, length), slice(None))
+
+        return second, wide, narrow
+
+    def stream(name, first, start, rows, refs):
+        second, wide, narrow = indices(first, start)
+        left = [c for step in chunk_order(sizes[first]) for c in step]
 
         def base(dest):
-            step, way = left.pop(0)
-            links.arrive((tag, step, way))
+            links.arrive((name, "core") + left.pop(0))
 
         base.ref = dense_ref
-        base.index = lambda *key: with_core(at(*key), core)
-        return base
-
-    def divided(offset):
+        base.index = lambda *key: with_core(wide(*key), core)
+
         def store(l, lo, index, total):
-            start, end = offset + lo, offset + lo + total.shape[0]
-            while start < end:
-                box = start // band
+            begin, end = start + lo, start + lo + total.shape[0]
+            while begin < end:
+                box = begin // band
                 stop = min(end, (box + 1) * band)
-                part = total[start - offset - lo : stop - offset - lo] / total_ref[pl.ds(box, 1), :]
+                part = total[begin - start - lo : stop - start - lo] / total_ref[pl.ds(box, 1), :]
                 part = part.astype(jnp.bfloat16)
-                all_ref[x, z, core, pl.ds(start, stop - start), :] = part
-                coadd_ref[pl.ds(start - box * band, stop - start), pl.ds(box * TILE, TILE)] = part
-                start = stop
-
-        return store
-
-    a_first = ring_reduce(
-        links, "a z", depth, z, width, split, a_at, held_ref, az_ref, az_half, lambda w: along[w],
-        base_of("core a", zs, a_at), None,
-    )
-    b_first = ring_reduce(
-        links, "b x", width, x, depth, rest, b_at, held_ref, bx_ref, bx_half, lambda w: beside[w],
-        base_of("core b", xs, b_at), None,
-    )
-    a_second = ring_reduce(
-        links, "a x", width, x, 1, split, a_next, held_ref, ax_ref, ax_half, lambda w: beside[w], None, divided(0)
-    )
-    b_second = ring_reduce(
-        links, "b z", depth, z, 1, rest, b_next, held_ref, bz_ref, bz_half, lambda w: along[w], None, divided(split)
-    )
-
-    def a_view(origin, lo, length):
-        return all_ref.at[:, origin, core, pl.ds(lo, length), :]
-
-    def b_view(origin, lo, length):
-        return all_ref.at[origin, :, core, pl.ds(split + lo, length), :]
-
-    def a_own(origin, lo, length):
-        return all_ref.at[origin, z, core, pl.ds(lo, length), :]
-
-    def b_own(origin, lo, length):
-        return all_ref.at[x, origin, core, pl.ds(split + lo, length), :]
-
-    def nothing(origin, key):
-        return None
-
-    def across(tag, view, length):
-        def arrived(origin, key):
-            links.start((tag, key), view(origin, 0, length), view(origin, 0, length), other)
-
-        return arrived
-
-    a_third = ring_gather(links, "a gather x", width, x, split, a_own, lambda w: beside[w], nothing)
-    b_third = ring_gather(links, "b gather z", depth, z, rest, b_own, lambda w: along[w], nothing)
-    a_last = ring_gather(
-        links, "a gather z", depth, z, split, a_view, lambda w: along[w], across("core a back", a_view, split)
-    )
-    b_last = ring_gather(
-        links, "b gather x", width, x, rest, b_view, lambda w: beside[w], across("core b back", b_view, rest)
-    )
-
-    def chain(*parts):
-        for part in parts:
-            yield from part
-
-    a_run = chain(a_first, a_second, a_third, a_last)
-    b_run = chain(b_first, b_second, b_third, b_last)
-    order = "ba" "a" "b" "aa" "ba" "baba" "bab" "bab" "abab" "b" "aabaabaab"
-    runs = {"a": a_run, "b": b_run}
-    for name in order:
+                all_ref[x, z, core, pl.ds(begin, stop - begin), :] = part
+                coadd_ref[pl.ds(begin - box * band, stop - begin), pl.ds(box * TILE, TILE)] = part
+                begin = stop
+
+        def view(maker):
+            return lambda origin, lo, length: all_ref.at[with_core(maker(origin, None, lo, length), core)]
+
+        def nothing(origin, key):
+            return None
+
+        def across(origin, key):
+            place = view(wide)(origin, 0, rows)
+            links.start((name, "back", key), place, place, other)
+
+        yield from ring_reduce(
+            links, (name, 1), sizes[first], places[first], sizes[second], rows, wide, held_ref,
+            refs[0], refs[1], lambda w: ways[first][w], base, None,
+        )
+        yield from ring_reduce(
+            links, (name, 2), sizes[second], places[second], 1, rows, narrow, held_ref,
+            refs[2], refs[3], lambda w: ways[second][w], None, store,
+        )
+        yield from ring_gather(
+            links, (name, 3), sizes[second], places[second], rows, view(narrow), lambda w: ways[second][w], nothing
+        )
+        yield from ring_gather(
+            links, (name, 4), sizes[first], places[first], rows, view(wide), lambda w: ways[first][w], across
+        )
+
+    firsts = {name: (first, start, rows) for name, first, start, rows in STREAMS}
+    waiting = {name: chunk_order(sizes[firsts[name][0]]) for name in firsts}
+    for name in ORDER:
+        if not waiting[name]:
+            continue
+        first, start, rows = firsts[name]
+        wide = indices(first, start)[1]
+        for step, way in waiting[name].pop(0):
+            index = wide(signed(places[first], step, way, sizes[first]), None, 0, rows)
+            links.start((name, "core", step, way), dense_ref.at[with_core(index, 1 - core)], held_ref.at[index], other)
+
+    runs = {}
+    for number, (name, first, start, rows) in enumerate(STREAMS):
+        runs[name] = stream(name, first, start, rows, buffers[4 * number : 4 * number + 4])
+    for name in ORDER:
         next(runs[name], None)
     for run in runs.values():
         for _ in run:
             pass
     for key in list(links.copies):
-        if key[0] in ("core a back", "core b back"):
+        if key[1] == "back":
             links.arrive(key)
     links.finish()
 
 
-def exchange(totals, dense, band, width, depth, split):
+def exchange(totals, dense, band, width, depth):
     rows = dense.shape[3]
-    rest = rows - split
-    copies = 2 * (2 * width + 2 * depth + 4) + 16
-
-    def buffers(size, lead, length):
-        return [
-            pltpu.VMEM((size // 2 - 1, 2, lead, length, TILE), jnp.bfloat16),
-            pltpu.VMEM((2, lead, length // 2, TILE), jnp.bfloat16),
-        ]
-
+    sizes = {"x": width, "z": depth}
+    copies = 0
+    scratch = []
+    for name, first, start, length in STREAMS:
+        size, other = sizes[first], width + depth - sizes[first]
+        copies += 4 * (size + other) + 2 * size
+        for places, lead in ((size, other), (other, 1)):
+            scratch.append(pltpu.VMEM((places // 2 - 1, 2, lead, length, TILE), jnp.bfloat16))
+            scratch.append(pltpu.VMEM((2, lead, length // 2, TILE), jnp.bfloat16))
     return pl.pallas_call(
-        functools.partial(exchange_kernel, width, depth, split),
+        functools.partial(exchange_kernel, width, depth),
         in_specs=[pl.BlockSpec(memory_space=pltpu.VMEM)] * 2,
         out_specs=[pl.BlockSpec(memory_space=pltpu.VMEM)] * 2,
         out_shape=[
             jax.ShapeDtypeStruct(dense.shape, jnp.bfloat16),
             jax.ShapeDtypeStruct((band, rows // band * TILE), jnp.bfloat16),
         ],
-        scratch_shapes=[pltpu.VMEM((width, depth, rows, TILE), jnp.bfloat16)]
-        + buffers(depth, width, split)
-        + buffers(width, 1, split)
-        + buffers(width, depth, rest)
-        + buffers(depth, 1, rest)
-        + [pltpu.SemaphoreType.DMA((copies,)), pltpu.SemaphoreType.DMA((copies,))],
+        scratch_shapes=[
+            pltpu.VMEM((width, depth, rows, TILE), jnp.bfloat16),
+            pltpu.SemaphoreType.DMA((copies,)),
+            pltpu.SemaphoreType.DMA((copies,)),
+        ]
+        + scratch,
         compiler_params=pltpu.CompilerParams(
             collective_id=0, has_side_effects=True, vmem_limit_bytes=40 << 20
         ),
@@ -510,8 +466,9 @@
     images_hbm,
     rows_hbm,
     cols_hbm,
+    out_hbm,
+    total_ref,
     out_ref,
-    total_ref,
     images_ref,
     rows_ref,
     cols_ref,
@@ -521,6 +478,7 @@
     left_ref,
     table_ref,
     load_ref,
+    save_ref,
     send_ref,
     recv_ref,
 ):
@@ -555,6 +513,10 @@
     def edge(image, way):
         start = band - HALO if way == 0 else 0
         return remote(4 + way, image, rows_hbm.at[image, pl.ds(start, HALO), :], halo_ref.at[image, way], way)
+
+    def save(image):
+        slot = lax.rem(image, 2)
+        return pltpu.make_async_copy(out_ref.at[slot], out_hbm.at[image], save_ref.at[slot])
 
     for kind in range(3):
         @pl.loop(0, count)
@@ -610,7 +572,15 @@
             warped = jnp.concatenate(
                 [warped[:HALO] * first, warped[HALO : HALO + band], warped[HALO + band :] * last], axis=0
             )
-            convolve(warped, reach, window_ref, left_ref, table_ref, out_ref, image, offsets)
+            @pl.when(image >= 2)
+            def _():
+                save(image - 2).wait()
+
+            convolve(warped, reach, window_ref, left_ref, table_ref, out_ref, lax.rem(image, 2), offsets)
+            save(image).start()
+
+    for image in (count - 2, count - 1):
+        save(image).wait()
 
     @pl.loop(0, count)
     def _(image):
@@ -631,12 +601,13 @@
     return pl.pallas_call(
         functools.partial(gather_match_kernel, reach, offsets),
         in_specs=[vmem, vmem, vmem, vmem, vmem, smem, vmem, hbm, hbm, hbm],
-        out_specs=[vmem, vmem],
+        out_specs=[hbm, vmem],
         out_shape=[
             jax.ShapeDtypeStruct((count, tiles, band, TILE), jnp.float32),
             jax.ShapeDtypeStruct((8, TILE), jnp.float32),
         ],
         scratch_shapes=[
+            pltpu.VMEM((2, tiles, band, TILE), jnp.float32),
             pltpu.VMEM((count, band, side), jnp.bfloat16),
             pltpu.VMEM((count, band, side), jnp.bfloat16),
             pltpu.VMEM((count, side, side), jnp.bfloat16),
@@ -646,11 +617,12 @@
             pltpu.VMEM((2 * tiles * (band // GROUP), offsets * TILE), jnp.bfloat16),
             pltpu.VMEM((offsets * TILE, 2 * TILE), jnp.bfloat16),
             pltpu.SemaphoreType.DMA((3, count)),
+            pltpu.SemaphoreType.DMA((2,)),
             pltpu.SemaphoreType.DMA((6, count)),
             pltpu.SemaphoreType.DMA((6, count)),
         ],
         compiler_params=pltpu.CompilerParams(
-            collective_id=1, has_side_effects=True, vmem_limit_bytes=46 << 20
+            collective_id=1, has_side_effects=True, vmem_limit_bytes=58 << 20
         ),
         name="gather_match",
     )(coef, taps, patch, block, index, levels, home, images, rows, cols)
@@ -694,7 +666,7 @@
     depth = DEPTH
     width = patches // (2 * depth)
     shape = (width, depth, 2, tiles * band, TILE)
-    templates, coadd = exchange(totals, dense.reshape(shape), band, width, depth, SPLIT)
+    templates, coadd = exchange(totals, dense.reshape(shape), band, width, depth)
     difference, coadd = subtract(targets, matched, templates.reshape(patches * tiles, band, TILE), coadd)
     return (difference.reshape(dets, visits, band, cols), coadd[None])
 

time: 156 us -> 136 us (0.87)
  Pallas kernels: 147 us -> 132 us
  local copies, waits for them, and re-layouts: 6.77 us -> 1.77 us
    pallas_call x1, Pallas kernels: 81.2 us -> 67.4 us  [exchange(): pl.pallas_call(functools.partial(exchange_kernel, width, depth), in_specs...]
    unnamed x16, local copies, waits for them, and re-layouts: 6.77 us -> 1.77 us
where the time goes in v5:
time: 136 us
  Pallas kernels  132 us (97%)
  local copies, waits for them, and re-layouts  1.77 us (1%)
    pallas_call x1, Pallas kernels, exchange(): pl.pallas_call(functools.partial(exchange_kernel, width, depth), in_specs...  67.4 us
    pallas_call x1, Pallas kernels, gather_match(): pl.pallas_call(functools.partial(gather_match_kernel, reach, offsets), in...  59 us
    pallas_call x1, Pallas kernels, collect(): pl.pallas_call(functools.partial(collect_kernel, (images // index.shape[0...  2.98 us

profile of v5, /device:TPU:1, one launch (start us, length us, event | category | flops | bytes accessed | tf_op | source)
XLA Modules:
  0.0 135.7 jit_solution(9673325828839941217)
XLA Ops:
  0.6 1.4 reduce
  2.0 0.0 copy-start.2
  2.0 0.0 copy-start.3
  2.0 0.0 copy-start.4
  2.0 0.0 copy-start.6
  2.0 0.0 copy-start.7
  2.0 59.0 %gather_match.1 = (f32[18,3,96,128]{3,2,1,0:T(8,128)}, f32[8,128]{1,0:T(8,128)}) custom-call(f32[6,3,21]{2,1,0:T(4,128)} %coef_ref.1, f32[21,21]{1,0:T(8,128)} %taps_ref.1, s32[27,128]{1,0:T(8,128)} %bitcast.13, s32[27,128]{1,0:T(8,128)} %bitcast.15, s32[3,384]{1,0:T(4,128)} %bitcast.17, f32[8]{0:T(128)} %levels_ref.3, s32[1,64]{1,0:T(1,128)} %bitcast.19, ...), custom_call_target="tpu_custom_call" | custom-call | tf_op jit(solution)/shard_map/gather_match/pallas_call | solution.py:601
  61.1 0.0 copy-done.2
  61.1 0.0 copy-done.3
  61.1 0.0 copy-done.4
  61.1 0.0 copy-done.6
  61.1 0.0 copy-done.7
  61.1 0.0 copy-start
  61.1 1.7 %copy-done = f32[18,3,96,128]{3,2,1,0:T(8,128)S(1)} copy-done((f32[18,3,96,128]{3,2,1,0:T(8,128)S(1)}, f32[18,3,96,128]{3,2,1,0:T(8,128)}, u32[]{:S(2)}) %copy-start) | copy-done | bytes 2654232
  62.9 0.0 copy-start.5
  62.9 3.0 %collect.1 = (bf16[192,96,128]{2,1,0:T(8,128)(2,1)S(1)}, s32[54]{0:T(128)S(1)}) custom-call(s32[27,128]{1,0:T(8,128)S(1)} %bitcast.14, s32[27,128]{1,0:T(8,128)S(1)} %bitcast.16, s32[3,384]{1,0:T(4,128)S(1)} %bitcast.18, f32[8]{0:T(128)S(1)} %copy-done.6, s32[64]{0:T(128)S(1)} %copy-done.7, f32[18,3,96,128]{3,2,1,0:T(8,128)S(1)} %copy-done), custom_call_target="tpu_custom_call" | custom-call | tf_op jit(solution)/shard_map/collect/pallas_call | solution.py:158
  65.9 0.0 copy-start.1
  65.9 0.0 copy-done.5
  65.9 67.4 %exchange.1 = (bf16[4,8,2,288,128]{4,3,2,1,0:T(8,128)(2,1)S(1)}, bf16[96,384]{1,0:T(8,128)(2,1)S(1)}) custom-call(f32[8,128]{1,0:T(8,128)S(1)} %copy-done.5, bf16[4,8,2,288,128]{4,3,2,1,0:T(8,128)(2,1)S(1)} %bitcast.12), custom_call_target="tpu_custom_call" | custom-call | tf_op jit(solution)/shard_map/exchange/pallas_call | solution.py:435
  133.3 0.0 copy-done.1
  133.3 2.4 %subtract.1 = (bf16[18,96,384]{2,1,0:T(8,128)(2,1)}, bf16[96,384]{1,0:T(8,128)(2,1)}) custom-call(s32[54]{0:T(128)S(1)} %get-tuple-element.11.target_ref, f32[18,3,96,128]{3,2,1,0:T(8,128)S(1)} %copy-done.1, bf16[192,96,128]{2,1,0:T(8,128)(2,1)S(1)} %bitcast.11, bf16[96,384]{1,0:T(8,128)(2,1)S(1)} %get-tuple-element.15.coadd_ref), custom_call_target="tpu_custom_call" | custom-call | tf_op jit(solution)/shard_map/subtract/pallas_call | solution.py:191
Async XLA Ops:
  2.0 59.1 %copy-start.2 = (s32[3456]{0:T(1024)S(1)}, s32[3456]{0:T(1024)}, u32[]{:S(2)}) copy-start(s32[3456]{0:T(1024)} %reduce) | copy-start | bytes 41476
  2.0 59.1 %copy-start.3 = (s32[3456]{0:T(1024)S(1)}, s32[3456]{0:T(1024)}, u32[]{:S(2)}) copy-start(s32[3456]{0:T(1024)} %param.16) | copy-start | bytes 41476
  2.0 59.1 %copy-start.4 = (s32[384,3]{0,1:T(4,128)S(1)}, s32[384,3]{0,1:T(4,128)}, u32[]{:S(2)}) copy-start(s32[384,3]{0,1:T(4,128)} %param.17) | copy-start | bytes 13828
  2.0 59.1 %copy-start.6 = (f32[8]{0:T(128)S(1)}, f32[8]{0:T(128)}, u32[]{:S(2)}) copy-start(f32[8]{0:T(128)} %levels_ref.3) | copy-start | bytes 100
  2.0 59.1 %copy-start.7 = (s32[64]{0:T(128)S(1)}, s32[64]{0:T(128)}, u32[]{:S(2)}) copy-start(s32[64]{0:T(128)} %home_ref.1) | copy-start | bytes 772
  61.1 1.8 %copy-start = (f32[18,3,96,128]{3,2,1,0:T(8,128)S(1)}, f32[18,3,96,128]{3,2,1,0:T(8,128)}, u32[]{:S(2)}) copy-start(f32[18,3,96,128]{3,2,1,0:T(8,128)} %get-tuple-element.10.matched_ref) | copy-start | bytes 7962628
  62.9 3.0 %copy-start.5 = (f32[8,128]{1,0:T(8,128)S(1)}, f32[8,128]{1,0:T(8,128)}, u32[]{:S(2)}) copy-start(f32[8,128]{1,0:T(8,128)} %get-tuple-element.12.total_ref) | copy-start | bytes 12292
  65.9 67.4 %copy-start.1 = (f32[18,3,96,128]{3,2,1,0:T(8,128)S(1)}, f32[18,3,96,128]{3,2,1,0:T(8,128)}, u32[]{:S(2)}) copy-start(f32[18,3,96,128]{3,2,1,0:T(8,128)} %get-tuple-element.10.matched_ref) | copy-start | bytes 7962628

commit v6 on v5

--- a/solution.py
+++ b/solution.py
@@ -12,8 +12,8 @@
 HALO = 16
 GROUP = 4
 DEPTH = 8
-STREAMS = (("a", "z", 0, 64), ("c", "z", 64, 64), ("b", "x", 128, 96), ("d", "x", 224, 64))
-ORDER = "bcdacbaacdbbabddcaabdaccbdaacbbdabccddabacdbccdbbadcaddcbcadbacd"
+STREAMS = (("a", "z", 0, 32), ("c", "z", 32, 64), ("b", "x", 96, 64), ("d", "x", 160, 64), ("e", "x", 224, 64))
+ORDER = "bcedbadecbadbecadcbeadcbeacdabecdaecdbaecbdea"
 PASS_ON = 2
 LAG = 4
 SUBTRACT_STEPS = 3
@@ -79,7 +79,9 @@
         weight = jnp.zeros((groups, TILE), jnp.float32)
         for n in range(table_ref.shape[0]):
             weight = jnp.where(level == float(n), table_ref[n], weight)
-        patch = jnp.concatenate([patch_ref[pl.ds(g * period + k, 1), :] for g in range(groups)], axis=0)
+        patch = jnp.concatenate(
+            [patch_ref[:, pl.ds((g * period + k) * TILE, TILE)] for g in range(groups)], axis=0
+        )
         block = jnp.concatenate([block_ref[pl.ds(g * period + k, 1), :] for g in range(groups)], axis=0)
         for box in range(boxes):
             sums[box] = sums[box] + jnp.where((patch == mine) & (block == box), weight, 0.0)
@@ -144,7 +146,7 @@
                 local = (det * visits + visit) * tiles + tile
                 piece = me * dets * visits * tiles + local
                 row, lane = piece // TILE, lax.rem(piece, TILE)
-                target = home_ref[patch_ref[row, lane]] * tiles + block_ref[row, lane]
+                target = home_ref[patch_ref[0, piece]] * tiles + block_ref[row, lane]
                 target_ref[local] = target
                 value = (weight * matched_ref[det * visits + visit, tile]).astype(jnp.bfloat16)
                 held = dense_ref[target].astype(jnp.float32)
@@ -239,16 +241,14 @@
     return lax.rem(place + size + (step if way == 0 else -step), size)
 
 
-def ring_reduce(links, tag, size, place, lead, rows, at, held_ref, whole_ref, half_ref, neighbour, base, finish):
-    middle, half = size // 2, rows // 2
-
+def adder(dest_at, lead, half, held_ref, base):
     def add(dest, extras, store):
         if base is not None:
             base(dest)
 
         def body(l, carry):
             for lo in (0, half):
-                index = at(dest, l, lo, half)
+                index = dest_at(dest, l, lo, half)
                 total = held_ref[index].astype(jnp.float32)
                 if base is not None:
                     total = total + base.ref[base.index(dest, l, lo, half)].astype(jnp.float32)
@@ -262,54 +262,90 @@
 
         lax.fori_loop(0, lead, body, 0)
 
+    return add
+
+
+def ring_reduce(links, tag, size, place, lead, rows, at, held_ref, whole_ref, half_ref, device, base, finish):
+    middle, half = size // 2, rows // 2
+    add = adder(at, lead, half, held_ref, base)
+
     def put(l, lo, index, total):
         held_ref[index] = total.astype(jnp.bfloat16)
 
+    def send(key, dest, buffer, way, distance, lo=0, length=rows):
+        links.start((tag, way, key), held_ref.at[at(dest, None, lo, length)], buffer, device(way, distance))
+
+    relay = middle // 2
     far = signed(place, middle, 0, size)
     if base is not None:
         add(far, [], put)
     for way in (0, 1):
-        links.start((tag, way, middle), held_ref.at[at(far, None, way * half, half)], half_ref.at[way], neighbour(way))
-    yield
+        send(middle, far, half_ref.at[way], way, relay, way * half, half)
     for step in range(middle - 1, 0, -1):
+        if step == relay:
+            continue
         for way in (0, 1):
             dest = signed(place, step, way, size)
-            links.arrive((tag, way, step + 1))
-            source = (half_ref, way, True) if step + 1 == middle else (whole_ref.at[step], way, False)
-            add(dest, [source], put)
-            links.start(
-                (tag, way, step), held_ref.at[at(dest, None, 0, rows)], whole_ref.at[step - 1, way], neighbour(way)
-            )
-        yield
+            if base is not None:
+                add(dest, [], put)
+            send(step, dest, whole_ref.at[step - 1, way], way, step - relay if step > relay else step)
+    yield
     for way in (0, 1):
-        links.arrive((tag, way, 1))
-    add(place, [(whole_ref.at[0], 0, False), (whole_ref.at[0], 1, False)], put if finish is None else finish)
+        dest = signed(place, relay, way, size)
+        sources = [(half_ref, way, True)]
+        links.arrive((tag, way, middle))
+        for step in range(relay + 1, middle):
+            links.arrive((tag, way, step))
+            sources.append((whole_ref.at[step - 1], way, False))
+        add(dest, sources, put)
+        send(relay, dest, whole_ref.at[relay - 1, way], way, relay)
     yield
-
-
-def ring_gather(links, tag, size, place, rows, view, neighbour, arrived):
+    last = [(step, way) for step in range(1, relay + 1) for way in (0, 1)]
+    for step, way in last:
+        links.arrive((tag, way, step))
+    add(place, [(whole_ref.at[step - 1], way, False) for step, way in last], put if finish is None else finish)
+
+
+def ring_gather(links, tag, size, place, rows, view, device, arrived):
     middle, half = size // 2, rows // 2
-    for way in (0, 1):
-        links.start((tag, way, 1), view(place, 0, rows), view(place, 0, rows), neighbour(way))
+    relay = middle // 2
+
+    def send(key, origin, way, distance, lo=0, length=rows):
+        part = view(origin, lo, length)
+        links.start((tag, way, key), part, part, device(way, distance))
+
+    for step in range(relay, 0, -1):
+        for way in (0, 1):
+            send(step, place, way, step)
     arrived(place, 0)
     yield
+    for way in (0, 1):
+        origin = signed(place, relay, 1 - way, size)
+        links.arrive((tag, way, relay))
+        for step in range(relay + 1, middle):
+            send(step, origin, way, step - relay)
+        send(middle, origin, way, relay, way * half, half)
+        arrived(origin, (relay, way))
     for step in range(1, middle):
+        if step < relay:
+            for way in (0, 1):
+                links.arrive((tag, way, step))
+                arrived(signed(place, step, 1 - way, size), (step, way))
+    yield
+    for step in range(relay + 1, middle):
         for way in (0, 1):
-            origin = signed(place, step, 1 - way, size)
             links.arrive((tag, way, step))
-            lo, length = (0, rows) if step + 1 < middle else (way * half, half)
-            links.start((tag, way, step + 1), view(origin, lo, length), view(origin, lo, length), neighbour(way))
-            arrived(origin, (step, way))
-        yield
+            arrived(signed(place, step, 1 - way, size), (step, way))
     for way in (0, 1):
         links.arrive((tag, way, middle))
     arrived(signed(place, middle, 0, size), middle)
-    yield
 
 
 def chunk_order(size):
     middle = size // 2
-    return [[(middle, 0)]] + [[(step, 0), (step, 1)] for step in range(middle - 1, 0, -1)] + [[(0, 0)]]
+    relay = middle // 2
+    first = [(middle, 0)] + [(step, way) for step in range(middle - 1, 0, -1) if step != relay for way in (0, 1)]
+    return [first, [(relay, 0), (relay, 1)], [(0, 0)]]
 
 
 def exchange_kernel(width, depth, total_ref, dense_ref, all_ref, coadd_ref, held_ref, send_ref, recv_ref, *buffers):
@@ -319,13 +355,17 @@
     z = lax.rem(me // 2, depth)
     x = me // (2 * depth)
     other = {"det": det_index(x, z, 1 - core, depth)}
-    ways = {
-        "x": [{"det": det_index(signed(x, 1, way, width), z, core, depth)} for way in (0, 1)],
-        "z": [{"det": det_index(x, signed(z, 1, way, depth), core, depth)} for way in (0, 1)],
-    }
+
+    def device(axis):
+        if axis == "x":
+            return lambda way, step: {"det": det_index(signed(x, step, way, width), z, core, depth)}
+        return lambda way, step: {"det": det_index(x, signed(z, step, way, depth), core, depth)}
+
     sizes, places = {"x": width, "z": depth}, {"x": x, "z": z}
     barrier = pltpu.get_barrier_semaphore()
-    friends = [other] + ways["x"] + ways["z"]
+    friends = [other]
+    for axis, size in (("x", width), ("z", depth)):
+        friends += [device(axis)(way, step) for step in range(1, size // 4 + 1) for way in (0, 1)]
     for friend in friends:
         pl.semaphore_signal(barrier, inc=1, device_id=friend, device_id_type=pl.DeviceIdType.MESH)
     pl.semaphore_wait(barrier, len(friends))
@@ -383,17 +423,17 @@
 
         yield from ring_reduce(
             links, (name, 1), sizes[first], places[first], sizes[second], rows, wide, held_ref,
-            refs[0], refs[1], lambda w: ways[first][w], base, None,
+            refs[0], refs[1], device(first), base, None,
         )
         yield from ring_reduce(
             links, (name, 2), sizes[second], places[second], 1, rows, narrow, held_ref,
-            refs[2], refs[3], lambda w: ways[second][w], None, store,
+            refs[2], refs[3], device(second), None, store,
         )
         yield from ring_gather(
-            links, (name, 3), sizes[second], places[second], rows, view(narrow), lambda w: ways[second][w], nothing
+            links, (name, 3), sizes[second], places[second], rows, view(narrow), device(second), nothing
         )
         yield from ring_gather(
-            links, (name, 4), sizes[first], places[first], rows, view(wide), lambda w: ways[first][w], across
+            links, (name, 4), sizes[first], places[first], rows, view(wide), device(first), across
         )
 
     firsts = {name: (first, start, rows) for name, first, start, rows in STREAMS}
@@ -645,7 +685,7 @@
     count = dets * visits
     patches = patch_home.shape[0]
     row_size = lax.axis_size("row")
-    patch = dest_patch.reshape(-1, TILE)
+    patch = dest_patch.T
     block = dest_block.reshape(-1, TILE)
     index = weight_index.T
 

time: 136 us -> 126 us (0.926)
  Pallas kernels: 132 us -> 123 us
    pallas_call x1, Pallas kernels: 67.4 us -> 58.5 us  [exchange(): pl.pallas_call(functools.partial(exchange_kernel, width, depth), in_specs...]
where the time goes in v6:
time: 126 us; the launch traced here: 125 us
  Pallas kernels  123 us (98%)
  local copies, waits for them, and re-layouts  1.77 us (1%)
    pallas_call x1, Pallas kernels, gather_match(): pl.pallas_call(functools.partial(gather_match_kernel, reach, offsets), in...  59 us
    pallas_call x1, Pallas kernels, exchange(): pl.pallas_call(functools.partial(exchange_kernel, width, depth), in_specs...  58.5 us
    pallas_call x1, Pallas kernels, collect(): pl.pallas_call(functools.partial(collect_kernel, (images // index.shape[0...  2.91 us

profile of v6, /device:TPU:1, one launch (start us, length us, event | category | flops | bytes accessed | tf_op | source)
XLA Modules:
  0.0 125.3 jit_solution(10336900442344633130)
XLA Ops:
  0.6 0.0 copy-start.2
  0.6 0.0 copy-start.3
  0.7 0.0 copy-start.4
  0.7 0.0 copy-start.6
  0.7 0.0 copy-start.7
  0.7 59.0 %gather_match.1 = (f32[18,3,96,128]{3,2,1,0:T(8,128)}, f32[8,128]{1,0:T(8,128)}) custom-call(f32[6,3,21]{2,1,0:T(4,128)} %coef_ref.1, f32[21,21]{1,0:T(8,128)} %taps_ref.1, s32[1,3456]{1,0:T(1,128)} %bitcast.15, s32[27,128]{1,0:T(8,128)} %bitcast.13, s32[3,384]{1,0:T(4,128)} %bitcast.17, f32[8]{0:T(128)} %levels_ref.3, s32[1,64]{1,0:T(1,128)} %bitcast.19, ...), custom_call_target="tpu_custom_call" | custom-call | tf_op jit(solution)/shard_map/gather_match/pallas_call | solution.py:641
  59.7 0.0 copy-done.2
  59.7 0.0 copy-done.3
  59.7 0.0 copy-done.4
  59.7 0.0 copy-done.6
  59.7 0.0 copy-done.7
  59.7 0.0 copy-start
  59.7 1.7 %copy-done = f32[18,3,96,128]{3,2,1,0:T(8,128)S(1)} copy-done((f32[18,3,96,128]{3,2,1,0:T(8,128)S(1)}, f32[18,3,96,128]{3,2,1,0:T(8,128)}, u32[]{:S(2)}) %copy-start) | copy-done | bytes 2654232
  61.5 0.0 copy-start.5
  61.5 2.9 %collect.1 = (bf16[192,96,128]{2,1,0:T(8,128)(2,1)S(1)}, s32[54]{0:T(128)S(1)}) custom-call(s32[1,3456]{1,0:T(1,128)S(1)} %bitcast.16, s32[27,128]{1,0:T(8,128)S(1)} %bitcast.14, s32[3,384]{1,0:T(4,128)S(1)} %bitcast.18, f32[8]{0:T(128)S(1)} %copy-done.6, s32[64]{0:T(128)S(1)} %copy-done.7, f32[18,3,96,128]{3,2,1,0:T(8,128)S(1)} %copy-done), custom_call_target="tpu_custom_call" | custom-call | tf_op jit(solution)/shard_map/collect/pallas_call | solution.py:160
  64.4 0.0 copy-start.1
  64.4 0.0 copy-done.5
  64.4 58.5 %exchange.1 = (bf16[4,8,2,288,128]{4,3,2,1,0:T(8,128)(2,1)S(1)}, bf16[96,384]{1,0:T(8,128)(2,1)S(1)}) custom-call(f32[8,128]{1,0:T(8,128)S(1)} %copy-done.5, bf16[4,8,2,288,128]{4,3,2,1,0:T(8,128)(2,1)S(1)} %bitcast.12), custom_call_target="tpu_custom_call" | custom-call | tf_op jit(solution)/shard_map/exchange/pallas_call | solution.py:475
  122.9 0.0 copy-done.1
  122.9 2.4 %subtract.1 = (bf16[18,96,384]{2,1,0:T(8,128)(2,1)}, bf16[96,384]{1,0:T(8,128)(2,1)}) custom-call(s32[54]{0:T(128)S(1)} %get-tuple-element.11.target_ref, f32[18,3,96,128]{3,2,1,0:T(8,128)S(1)} %copy-done.1, bf16[192,96,128]{2,1,0:T(8,128)(2,1)S(1)} %bitcast.11, bf16[96,384]{1,0:T(8,128)(2,1)S(1)} %get-tuple-element.15.coadd_ref), custom_call_target="tpu_custom_call" | custom-call | tf_op jit(solution)/shard_map/subtract/pallas_call | solution.py:193
Async XLA Ops:
  0.6 59.1 %copy-start.2 = (s32[3456]{0:T(1024)S(1)}, s32[3456]{0:T(1024)}, u32[]{:S(2)}) copy-start(s32[3456]{0:T(1024)} %param.16) | copy-start | bytes 41476
  0.6 59.1 %copy-start.3 = (s32[3456,1]{0,1:T(1,128)S(1)}, s32[3456,1]{0,1:T(1,128)}, u32[]{:S(2)}) copy-start(s32[3456,1]{0,1:T(1,128)} %param.15) | copy-start | bytes 41476
  0.7 59.1 %copy-start.4 = (s32[384,3]{0,1:T(4,128)S(1)}, s32[384,3]{0,1:T(4,128)}, u32[]{:S(2)}) copy-start(s32[384,3]{0,1:T(4,128)} %param.17) | copy-start | bytes 13828
  0.7 59.1 %copy-start.6 = (f32[8]{0:T(128)S(1)}, f32[8]{0:T(128)}, u32[]{:S(2)}) copy-start(f32[8]{0:T(128)} %levels_ref.3) | copy-start | bytes 100
  0.7 59.1 %copy-start.7 = (s32[64]{0:T(128)S(1)}, s32[64]{0:T(128)}, u32[]{:S(2)}) copy-start(s32[64]{0:T(128)} %home_ref.1) | copy-start | bytes 772
  59.7 1.8 %copy-start = (f32[18,3,96,128]{3,2,1,0:T(8,128)S(1)}, f32[18,3,96,128]{3,2,1,0:T(8,128)}, u32[]{:S(2)}) copy-start(f32[18,3,96,128]{3,2,1,0:T(8,128)} %get-tuple-element.10.matched_ref) | copy-start | bytes 7962628
  61.5 2.9 %copy-start.5 = (f32[8,128]{1,0:T(8,128)S(1)}, f32[8,128]{1,0:T(8,128)}, u32[]{:S(2)}) copy-start(f32[8,128]{1,0:T(8,128)} %get-tuple-element.12.total_ref) | copy-start | bytes 12292
  64.4 58.5 %copy-start.1 = (f32[18,3,96,128]{3,2,1,0:T(8,128)S(1)}, f32[18,3,96,128]{3,2,1,0:T(8,128)}, u32[]{:S(2)}) copy-start(f32[18,3,96,128]{3,2,1,0:T(8,128)} %get-tuple-element.10.matched_ref) | copy-start | bytes 7962628

commit v7 on v6

--- a/solution.py
+++ b/solution.py
@@ -148,7 +148,8 @@
                 row, lane = piece // TILE, lax.rem(piece, TILE)
                 target = home_ref[patch_ref[0, piece]] * tiles + block_ref[row, lane]
                 target_ref[local] = target
-                value = (weight * matched_ref[det * visits + visit, tile]).astype(jnp.bfloat16)
+                value = matched_ref[det * visits + visit, tile].astype(jnp.float32)
+                value = (weight * value).astype(jnp.bfloat16)
                 held = dense_ref[target].astype(jnp.float32)
                 dense_ref[target] = (held + value.astype(jnp.float32)).astype(jnp.bfloat16)
 
@@ -183,7 +184,8 @@
         image = step * images + local
         for tile in range(tiles):
             template = template_ref[target_ref[image * tiles + tile]].astype(jnp.float32)
-            out_ref[local, :, pl.ds(tile * TILE, TILE)] = (matched_ref[image, tile] - template).astype(jnp.bfloat16)
+            value = matched_ref[image, tile].astype(jnp.float32) - template
+            out_ref[local, :, pl.ds(tile * TILE, TILE)] = value.astype(jnp.bfloat16)
 
 
 def subtract(targets, matched, templates, coadd):
@@ -509,6 +511,7 @@
     out_hbm,
     total_ref,
     out_ref,
+    saved_ref,
     images_ref,
     rows_ref,
     cols_ref,
@@ -556,7 +559,7 @@
 
     def save(image):
         slot = lax.rem(image, 2)
-        return pltpu.make_async_copy(out_ref.at[slot], out_hbm.at[image], save_ref.at[slot])
+        return pltpu.make_async_copy(saved_ref.at[slot], out_hbm.at[image], save_ref.at[slot])
 
     for kind in range(3):
         @pl.loop(0, count)
@@ -616,7 +619,8 @@
             def _():
                 save(image - 2).wait()
 
-            convolve(warped, reach, window_ref, left_ref, table_ref, out_ref, lax.rem(image, 2), offsets)
+            convolve(warped, reach, window_ref, left_ref, table_ref, out_ref, 0, offsets)
+            saved_ref[lax.rem(image, 2)] = out_ref[0].astype(jnp.bfloat16)
             save(image).start()
 
     for image in (count - 2, count - 1):
@@ -643,11 +647,12 @@
         in_specs=[vmem, vmem, vmem, vmem, vmem, smem, vmem, hbm, hbm, hbm],
         out_specs=[hbm, vmem],
         out_shape=[
-            jax.ShapeDtypeStruct((count, tiles, band, TILE), jnp.float32),
+            jax.ShapeDtypeStruct((count, tiles, band, TILE), jnp.bfloat16),
             jax.ShapeDtypeStruct((8, TILE), jnp.float32),
         ],
         scratch_shapes=[
-            pltpu.VMEM((2, tiles, band, TILE), jnp.float32),
+            pltpu.VMEM((1, tiles, band, TILE), jnp.float32),
+            pltpu.VMEM((2, tiles, band, TILE), jnp.bfloat16),
             pltpu.VMEM((count, band, side), jnp.bfloat16),
             pltpu.VMEM((count, band, side), jnp.bfloat16),
             pltpu.VMEM((count, side, side), jnp.bfloat16),

time: 126 us -> 125 us (level)
  no operation moved by 1% of the time
where the time goes in v7:
time: 125 us
  Pallas kernels  123 us (98%)
  local copies, waits for them, and re-layouts  1.34 us (1%)
    pallas_call x1, Pallas kernels, gather_match(): pl.pallas_call(functools.partial(gather_match_kernel, reach, offsets), in...  59 us
    pallas_call x1, Pallas kernels, exchange(): pl.pallas_call(functools.partial(exchange_kernel, width, depth), in_specs...  58.4 us
    pallas_call x1, Pallas kernels, collect(): pl.pallas_call(functools.partial(collect_kernel, (images // index.shape[0...  2.93 us

profile of v7, /device:TPU:1, one launch (start us, length us, event | category | flops | bytes accessed | tf_op | source)
XLA Modules:
  0.0 124.9 jit_solution(60328446903220511)
XLA Ops:
  0.6 0.0 copy-start.2
  0.6 0.0 copy-start.3
  0.7 0.0 copy-start.4
  0.7 0.0 copy-start.6
  0.7 0.0 copy-start.7
  0.7 59.0 %gather_match.1 = (bf16[18,3,96,128]{3,2,1,0:T(8,128)(2,1)}, f32[8,128]{1,0:T(8,128)}) custom-call(f32[6,3,21]{2,1,0:T(4,128)} %coef_ref.1, f32[21,21]{1,0:T(8,128)} %taps_ref.1, s32[1,3456]{1,0:T(1,128)} %bitcast.15, s32[27,128]{1,0:T(8,128)} %bitcast.13, s32[3,384]{1,0:T(4,128)} %bitcast.17, f32[8]{0:T(128)} %levels_ref.3, s32[1,64]{1,0:T(1,128)} %bitcast.19, ...), custom_call_target="tpu_custom_call" | custom-call | tf_op jit(solution)/shard_map/gather_match/pallas_call | solution.py:645
  59.7 0.0 copy-done.2
  59.7 0.0 copy-done.3
  59.8 0.0 copy-done.4
  59.8 0.0 copy-done.6
  59.8 0.0 copy-done.7
  59.8 0.0 copy-start
  59.8 1.3 %copy-done = bf16[18,3,96,128]{3,2,1,0:T(8,128)(2,1)S(1)} copy-done((bf16[18,3,96,128]{3,2,1,0:T(8,128)(2,1)S(1)}, bf16[18,3,96,128]{3,2,1,0:T(8,128)(2,1)}, u32[]{:S(2)}) %copy-start) | copy-done | bytes 1327128
  61.1 0.0 copy-start.5
  61.1 2.9 %collect.1 = (bf16[192,96,128]{2,1,0:T(8,128)(2,1)S(1)}, s32[54]{0:T(128)S(1)}) custom-call(s32[1,3456]{1,0:T(1,128)S(1)} %bitcast.16, s32[27,128]{1,0:T(8,128)S(1)} %bitcast.14, s32[3,384]{1,0:T(4,128)S(1)} %bitcast.18, f32[8]{0:T(128)S(1)} %copy-done.6, s32[64]{0:T(128)S(1)} %copy-done.7, bf16[18,3,96,128]{3,2,1,0:T(8,128)(2,1)S(1)} %copy-done), custom_call_target="tpu_custom_call" | custom-call | tf_op jit(solution)/shard_map/collect/pallas_call | solution.py:161
  64.0 0.0 copy-done.5
  64.1 0.0 copy-start.1
  64.1 58.4 %exchange.1 = (bf16[4,8,2,288,128]{4,3,2,1,0:T(8,128)(2,1)S(1)}, bf16[96,384]{1,0:T(8,128)(2,1)S(1)}) custom-call(f32[8,128]{1,0:T(8,128)S(1)} %copy-done.5, bf16[4,8,2,288,128]{4,3,2,1,0:T(8,128)(2,1)S(1)} %bitcast.12), custom_call_target="tpu_custom_call" | custom-call | tf_op jit(solution)/shard_map/exchange/pallas_call | solution.py:477
  122.5 0.0 copy-done.1
  122.5 2.4 %subtract.1 = (bf16[18,96,384]{2,1,0:T(8,128)(2,1)}, bf16[96,384]{1,0:T(8,128)(2,1)}) custom-call(s32[54]{0:T(128)S(1)} %get-tuple-element.11.target_ref, bf16[18,3,96,128]{3,2,1,0:T(8,128)(2,1)S(1)} %copy-done.1, bf16[192,96,128]{2,1,0:T(8,128)(2,1)S(1)} %bitcast.11, bf16[96,384]{1,0:T(8,128)(2,1)S(1)} %get-tuple-element.15.coadd_ref), custom_call_target="tpu_custom_call" | custom-call | tf_op jit(solution)/shard_map/subtract/pallas_call | solution.py:195
Async XLA Ops:
  0.6 59.1 %copy-start.2 = (s32[3456]{0:T(1024)S(1)}, s32[3456]{0:T(1024)}, u32[]{:S(2)}) copy-start(s32[3456]{0:T(1024)} %param.16) | copy-start | bytes 41476
  0.6 59.1 %copy-start.3 = (s32[3456,1]{0,1:T(1,128)S(1)}, s32[3456,1]{0,1:T(1,128)}, u32[]{:S(2)}) copy-start(s32[3456,1]{0,1:T(1,128)} %param.15) | copy-start | bytes 41476
  0.7 59.1 %copy-start.4 = (s32[384,3]{0,1:T(4,128)S(1)}, s32[384,3]{0,1:T(4,128)}, u32[]{:S(2)}) copy-start(s32[384,3]{0,1:T(4,128)} %param.17) | copy-start | bytes 13828
  0.7 59.1 %copy-start.6 = (f32[8]{0:T(128)S(1)}, f32[8]{0:T(128)}, u32[]{:S(2)}) copy-start(f32[8]{0:T(128)} %levels_ref.3) | copy-start | bytes 100
  0.7 59.1 %copy-start.7 = (s32[64]{0:T(128)S(1)}, s32[64]{0:T(128)}, u32[]{:S(2)}) copy-start(s32[64]{0:T(128)} %home_ref.1) | copy-start | bytes 772
  59.8 1.3 %copy-start = (bf16[18,3,96,128]{3,2,1,0:T(8,128)(2,1)S(1)}, bf16[18,3,96,128]{3,2,1,0:T(8,128)(2,1)}, u32[]{:S(2)}) copy-start(bf16[18,3,96,128]{3,2,1,0:T(8,128)(2,1)} %get-tuple-element.10.matched_ref) | copy-start | bytes 3981316
  61.1 2.9 %copy-start.5 = (f32[8,128]{1,0:T(8,128)S(1)}, f32[8,128]{1,0:T(8,128)}, u32[]{:S(2)}) copy-start(f32[8,128]{1,0:T(8,128)} %get-tuple-element.12.total_ref) | copy-start | bytes 12292
  64.1 58.4 %copy-start.1 = (bf16[18,3,96,128]{3,2,1,0:T(8,128)(2,1)S(1)}, bf16[18,3,96,128]{3,2,1,0:T(8,128)(2,1)}, u32[]{:S(2)}) copy-start(bf16[18,3,96,128]{3,2,1,0:T(8,128)(2,1)} %get-tuple-element.10.matched_ref) | copy-start | bytes 3981316
